TPU v7x, 32 devices: a whole 2x2x4 slice. The times are simulated.
32 devices in a mesh: src: 8 (over z, y), tm: 4 (over x, core).
Axes of the slice: x: 2, y: 2, z: 4, core: 2. Of those that a mesh axis runs over, the one named last changes fastest.
Arguments:
- green: bfloat16 [4, 1024, 128, 128], P('tm', 'src'), may hold values from -0.046875 to 0.046875
- block_rows: int32 [4, 1024], P('tm', 'src'), may hold values from 0 to 7
- block_cols: int32 [4, 1024], P('tm', 'src'), may hold values from 0 to 31
- block_live: int32 [4, 1024], P('tm', 'src'), may hold values from 0 to 1, as said below
- data: float32 [4, 1024, 128], P('tm', 'src'), may hold values from -6 to 6
- row_weight: float32 [4, 1024], P('tm', 'src'), may hold values from 0.3 to 9
- source_gain: float32 [32768], P('src'), may hold values from 0.2 to 3
Outputs:
- solution: float32 [32768, 128], P(('src', 'tm'))
- residual: float32 [4, 1024, 128], P('tm', 'src')
- misfit: float32 [2, 128], replicated
Inputs may be any that keep to these rules, and one draw needn't show every extreme that they name: `block_live`: within one device's 128 slots every slot is live with the same chance, a chance that differs from device to device; in some device all 128 slots are live.
All inputs are finite; a program needn't handle non-finite values.
Results may differ from a plain program's by a relative error of at most 0.0038.
Values may be sent and summed in bfloat16 or wider, within the bound.
No kernel may reach another device: no remote copies, remote signals or barrier semaphores. Data moves between devices by JAX's collectives and lax.ppermute only.
A program may use at most 128 MiB of HBM per device.

v0:
```python
import jax
import jax.numpy as jnp
from jax import lax
from jax.sharding import PartitionSpec as P

ITERS = 2


HIGH = lax.Precision.HIGHEST
EPSILON = 1e-06


def shards(green, block_rows, block_cols, block_live, data, row_weight, source_gain):
    blocks = green[0]
    slot_count = blocks.shape[0]
    block_size = blocks.shape[1]
    datasets = data.shape[2]
    own_rows = data.shape[1]
    own_blocks = own_rows // block_size
    groups = lax.axis_size("src")
    windows = lax.axis_size("tm")
    window_blocks = own_blocks * groups
    sources = source_gain.shape[0]
    col_blocks = sources // block_size
    share_rows = sources // windows
    total_rows = own_rows * groups * windows
    live_slots = block_live[0].astype(jnp.float32)[:, None]
    row_hit = block_rows[0][:, None] == jnp.arange(window_blocks, dtype=jnp.int32)[None, :]
    col_hit = block_cols[0][:, None] == jnp.arange(col_blocks, dtype=jnp.int32)[None, :]
    gather_rows = row_hit.astype(jnp.bfloat16)
    gather_cols = col_hit.astype(jnp.bfloat16)
    spread_rows = jnp.transpose(row_hit.astype(jnp.float32) * live_slots)
    spread_cols = jnp.transpose(col_hit.astype(jnp.float32) * live_slots)
    weight = row_weight[0][:, None]
    tm_index = lax.axis_index("tm")
    gain_group = source_gain[:, None]

    def adjoint(residual):
        sent = (weight * residual).astype(jnp.bfloat16).reshape(own_blocks, block_size * datasets)
        gathered = lax.all_gather(sent, "src", axis=0, tiled=True)
        picked = jnp.dot(gather_rows, gathered, preferred_element_type=jnp.bfloat16)
        products = jnp.einsum(
            "kac,kar->kcr",
            blocks,
            picked.reshape(slot_count, block_size, datasets),
            preferred_element_type=jnp.float32,
        )
        products = products.reshape(slot_count, block_size * datasets)
        return jnp.dot(spread_cols, products, precision=HIGH).reshape(sources, datasets)

    def steepest_of(residual):
        summed = lax.psum(adjoint(residual), "tm")
        steepest = gain_group * summed
        gamma_now = lax.psum(jnp.sum(steepest * steepest, axis=0), "src")
        return (steepest, gamma_now)

    residual = weight * data[0]
    steepest, gamma_now = steepest_of(residual)
    direction = steepest
    solution = jnp.zeros((share_rows, datasets), jnp.float32)
    square_sum = lax.psum(jnp.sum(residual * residual, axis=0), ("src", "tm"))
    misfits = []
    for iteration in range(ITERS):
        forward_picked = jnp.dot(
            gather_cols,
            (gain_group * direction)
            .astype(jnp.bfloat16)
            .reshape(col_blocks, block_size * datasets),
            preferred_element_type=jnp.bfloat16,
        )
        forward_products = jnp.einsum(
            "kac,kcr->kar",
            blocks,
            forward_picked.reshape(slot_count, block_size, datasets),
            preferred_element_type=jnp.float32,
        )
        forward_products = forward_products.reshape(slot_count, block_size * datasets)
        forward_summed = lax.psum_scatter(
            jnp.dot(spread_rows, forward_products, precision=HIGH),
            "src",
            scatter_dimension=0,
            tiled=True,
        )
        image = weight * forward_summed.reshape(own_rows, datasets)
        image_norm, cross_term = lax.psum(
            (jnp.sum(image * image, axis=0), jnp.sum(residual * image, axis=0)), ("src", "tm")
        )
        step_size = gamma_now / (image_norm + EPSILON)
        solution = solution + step_size * lax.dynamic_slice_in_dim(
            direction, tm_index * share_rows, share_rows, 0
        )
        residual = residual - step_size * image
        square_sum = square_sum - 2.0 * step_size * cross_term + step_size * step_size * image_norm
        misfits.append(square_sum / total_rows)
        if iteration + 1 < ITERS:
            steepest, gamma_next = steepest_of(residual)
            direction = steepest + gamma_next / (gamma_now + EPSILON) * direction
            gamma_now = gamma_next
    return (solution, residual[None], jnp.stack(misfits))


def solution(mesh):
    placed = (
        P("tm", "src", None, None),
        P("tm", "src"),
        P("tm", "src"),
        P("tm", "src"),
        P("tm", "src", None),
        P("tm", "src"),
        P("src"),
    )
    return jax.shard_map(
        shards,
        mesh=mesh,
        in_specs=placed,
        out_specs=(P(("src", "tm"), None), P("tm", "src", None), P()),
        check_vma=False,
    )
```

profile of v0, /device:TPU:0, one launch (start us, length us, event | category | flops | bytes accessed | tf_op | source)
XLA Modules:
  0.0 566.8 jit_solution(3843857328172715394)
XLA Ops:
  7.2 0.0 all-reduce.8.cloned.1.call-start
  7.2 0.7 mul.257
  7.9 0.9 convert_bitcast_fusion.1
  8.9 33.0 %all-gather = bf16[8,1,16384]{2,1,0:T(2,128)(2,1)S(1)} all-gather(bf16[1,1,16384]{2,1,0:T(2,128)(2,1)S(1)} %get-tuple-element.19), channel_id=1, replica_groups=mesh['src'=8,'tm'=4] {'src'}, dimensions={0}, use_global_device_ids=true | all-gather | bytes 294912 | tf_op jit(solution)/shard_map/all_gather | solution.py:40
  41.9 1.9 convolution_bitcast_fusion.1
  43.9 0.0 copy-start
  43.9 1.2 copy.42
  45.1 0.9 copy-done
  46.1 4.8 fusion.10
  50.8 9.3 %copy.27 = f32[128,128,128]{0,2,1:T(8,128)} copy(f32[128,128,128]{1,2,0:T(8,128)} %fusion.10) | data formatting | bytes 16777216 | tf_op jit(solution)/shard_map/kac,kar->kcr/dot_general | solution.py:42
  60.2 10.7 %fusion.50 = f32[32,16384]{1,0:T(8,128)S(1)} fusion(f32[128,16384]{0,1:T(8,128)} %bitcast.96, f32[128]{0:T(128)S(1)} %convert_bitcast_fusion.2, s32[128]{0:T(128)S(1)} %bitcast.119), kind=kOutput, calls=%fused_computation.57 | convolution fusion | flops 805314560 | bytes 10486784 | tf_op jit(solution)/shard_map/dot_general | solution.py:49
  70.9 0.0 copy-start.5
  70.9 1.5 reshape.248
  72.4 0.0 all-reduce.8.cloned.1.call-update
  72.4 0.2 all-reduce.12.cloned.1.call-start
  72.6 52.4 %all-reduce.8.cloned.1.call-done = f32[4096,128]{1,0:T(8,128)} async-done(((f32[4096,128]{1,0:T(8,128)}), f32[4096,128]{1,0:T(8,128)}) %all-reduce.8.cloned.1.call-update) | async-done | bytes 2097168 | tf_op jit(solution)/shard_map/psum | solution.py:52
  125.1 1.9 multiply_convert_fusion.1
  127.0 1.3 reshape.249
  128.3 2.7 fusion.29
  131.0 7.3 %fusion.13 = f32[128,128,128]{1,2,0:T(8,128)} fusion(bf16[1,128,128,128]{3,2,1,0:T(8,128)(2,1)S(1)} %copy-done.1, bf16[128,128,128]{2,0,1:T(8,128)(2,1)S(1)} %fusion.29), kind=kOutput, calls=%fused_computation.11 | convolution fusion | flops 536870912 | bytes 16777216 | tf_op jit(solution)/shard_map/kac,kcr->kar/dot_general | solution.py:71
  138.3 9.3 %copy.30 = f32[128,128,128]{0,2,1:T(8,128)} copy(f32[128,128,128]{1,2,0:T(8,128)} %fusion.13) | data formatting | bytes 16777216 | tf_op jit(solution)/shard_map/kac,kcr->kar/dot_general | solution.py:71
  147.6 10.1 %fusion.38 = f32[8,16384]{1,0:T(8,128)} fusion(f32[128,16384]{0,1:T(8,128)} %bitcast.98, f32[128]{0:T(128)S(1)} %convert_bitcast_fusion.2, s32[128]{0:T(128)S(1)} %bitcast.112), kind=kOutput, calls=%fused_computation.35 | convolution fusion | flops 201328640 | bytes 8913920 | tf_op jit(solution)/shard_map/dot_general | solution.py:79
  157.7 0.0 all-reduce.12.cloned.1.call-update
  157.7 0.0 all-reduce.10.cloned.1.call-start
  157.8 0.0 copy-done.10
  157.8 0.6 dynamic-slice
  158.4 0.6 multiply_reduce_fusion.1
  158.9 21.4 %psum.64 = f32[128]{0:T(128)S(1)} all-reduce(f32[128]{0:T(128)S(1)} %multiply_reduce_fusion.1), channel_id=1, replica_groups=mesh['src'=8,'tm'=4] {'src'}, use_global_device_ids=true, to_apply=%region_2.0 | all-reduce | flops 128 | bytes 1024 | tf_op jit(solution)/shard_map/psum | solution.py:54
  180.3 50.4 %all-reduce.12.cloned.1.call-done = f32[8,16384]{1,0:T(8,128)} async-done(((f32[8,16384]{1,0:T(8,128)}), f32[8,16384]{1,0:T(8,128)}) %all-reduce.12.cloned.1.call-update) | async-done | bytes 524304
  230.7 1.7 constant_dynamic-slice_fusion.1
  232.5 0.1 multiply_reduce_fusion.6
  232.6 39.4 %psum.65 = f32[128]{0:T(128)S(1)} all-reduce(f32[128]{0:T(128)S(1)} %multiply_reduce_fusion.6), channel_id=1, replica_groups=mesh['src'=8,'tm'=4] {'src','tm'}, use_global_device_ids=true, to_apply=%region_5.0 | all-reduce | flops 128 | bytes 1024 | tf_op jit(solution)/shard_map/psum | solution.py:85
  272.0 1.8 convert_bitcast_fusion
  273.8 31.5 %all-gather.1 = bf16[8,1,16384]{2,1,0:T(2,128)(2,1)S(1)} all-gather(bf16[1,1,16384]{2,1,0:T(2,128)(2,1)S(1)} %convert_bitcast_fusion), channel_id=1, replica_groups=mesh['src'=8,'tm'=4] {'src'}, dimensions={0}, use_global_device_ids=true | all-gather | bytes 294912 | tf_op jit(solution)/shard_map/all_gather | solution.py:40
  305.3 1.3 convolution_bitcast_fusion
  306.6 0.0 copy-start.2
  306.6 1.2 copy.43
  307.9 0.9 copy-done.2
  308.8 4.7 fusion.18
  313.6 9.4 %copy.32 = f32[128,128,128]{0,2,1:T(8,128)} copy(f32[128,128,128]{1,2,0:T(8,128)} %fusion.18) | data formatting | bytes 16777216 | tf_op jit(solution)/shard_map/kac,kar->kcr/dot_general | solution.py:42
  322.9 11.7 %fusion.48 = f32[32,16384]{1,0:T(8,128)} fusion(f32[128,16384]{0,1:T(8,128)} %bitcast.99, f32[128]{0:T(128)S(1)} %convert_bitcast_fusion.2, s32[128]{0:T(128)S(1)} %bitcast.121), kind=kOutput, calls=%fused_computation.55 | convolution fusion | flops 805314560 | bytes 10486784 | tf_op jit(solution)/shard_map/dot_general | solution.py:49
  334.6 2.7 reshape.254
  337.3 0.0 all-reduce.10.cloned.1.call-update
  337.3 0.0 all-reduce.14.cloned.1.call-start
  337.4 51.3 %all-reduce.10.cloned.1.call-done = f32[4096,128]{1,0:T(8,128)} async-done(((f32[4096,128]{1,0:T(8,128)}), f32[4096,128]{1,0:T(8,128)}) %all-reduce.10.cloned.1.call-update) | async-done | bytes 2097168 | tf_op jit(solution)/shard_map/psum | solution.py:52
  388.7 1.9 multiply_reduce_fusion
  390.7 21.6 %psum.67 = f32[128]{0:T(128)S(1)} all-reduce(f32[128]{0:T(128)S(1)} %multiply_reduce_fusion), channel_id=1, replica_groups=mesh['src'=8,'tm'=4] {'src'}, use_global_device_ids=true, to_apply=%region_8.0 | all-reduce | flops 128 | bytes 1024 | tf_op jit(solution)/shard_map/psum | solution.py:54
  412.3 3.3 multiply_convert_fusion
  415.5 1.5 reshape.255
  417.1 0.0 copy-start.3
  417.1 1.3 fusion.26
  418.4 0.9 copy-done.3
  419.2 7.3 %fusion.21 = f32[128,128,128]{1,2,0:T(8,128)} fusion(bf16[1,128,128,128]{3,2,1,0:T(8,128)(2,1)S(1)} %copy-done.3, bf16[128,128,128]{2,0,1:T(8,128)(2,1)S(1)} %fusion.26), kind=kOutput, calls=%fused_computation.13 | convolution fusion | flops 536870912 | bytes 16777216 | tf_op jit(solution)/shard_map/kac,kcr->kar/dot_general | solution.py:71
  426.5 9.3 %copy.35 = f32[128,128,128]{0,2,1:T(8,128)} copy(f32[128,128,128]{1,2,0:T(8,128)} %fusion.21) | data formatting | bytes 16777216 | tf_op jit(solution)/shard_map/kac,kcr->kar/dot_general | solution.py:71
  435.9 10.1 %fusion.36 = f32[8,16384]{1,0:T(8,128)} fusion(f32[128,16384]{0,1:T(8,128)} %bitcast.97, f32[128]{0:T(128)S(1)} %convert_bitcast_fusion.2, s32[128]{0:T(128)S(1)} %bitcast.114), kind=kOutput, calls=%fused_computation.33 | convolution fusion | flops 201328640 | bytes 8913920 | tf_op jit(solution)/shard_map/dot_general | solution.py:79
  446.0 0.0 all-reduce.14.cloned.1.call-update
  446.0 69.3 %all-reduce.14.cloned.1.call-done = f32[8,16384]{1,0:T(8,128)} async-done(((f32[8,16384]{1,0:T(8,128)}), f32[8,16384]{1,0:T(8,128)}) %all-reduce.14.cloned.1.call-update) | async-done | bytes 524304
  515.3 1.7 constant_dynamic-slice_fusion
  517.0 0.0 copy-done.4
  517.0 0.1 multiply_reduce_fusion.2
  517.1 39.5 %all-reduce.2 = (f32[128]{0:T(128)S(1)}, f32[128]{0:T(128)S(1)}, f32[128]{0:T(128)S(1)}, f32[128]{0:T(128)S(1)}) all-reduce(f32[128]{0:T(128)S(1)} %get-tuple-element.6, f32[128]{0:T(128)S(1)} %get-tuple-element.5, f32[128]{0:T(128)S(1)} %get-tuple-element.4, f32[128]{0:T(128)S(1)} %get-tuple-element.3), channel_id=1, replica_groups=mesh['src'=8,'tm'=4] {'src','tm'}, use_global_device_ids=true, to_apply=%region_11.0 | all-reduce | flops 512 | bytes 4096 | tf_op jit(solution)/shard_map/psum | solution.py:85
  556.6 0.6 pad_maximum_fusion
  557.2 0.7 multiply_subtract_fusion
  557.9 1.9 multiply_add_fusion.1
  (19 shorter events, 0.1 us)
Async XLA Ops:
  7.2 117.9 %all-reduce.8.cloned.1.call-start = ((), (), s32[]{:S(2)}) async-start(), calls=%async_computation | async-start | bytes 4194304 | tf_op jit(solution)/shard_map/psum | solution.py:52
  43.9 2.2 copy-start
  50.8 9.4 %copy-start.9 = (s32[1,128]{1,0:T(1,128)S(1)}, s32[1,128]{1,0:T(1,128)}, u32[]{:S(2)}) copy-start(s32[1,128]{1,0:T(1,128)} %param.10) | copy-start | bytes 1540
  50.8 9.4 %copy-start.8 = (s32[1,128]{1,0:T(1,128)S(1)}, s32[1,128]{1,0:T(1,128)}, u32[]{:S(2)}) copy-start(s32[1,128]{1,0:T(1,128)} %param.9) | copy-start | bytes 1540
  70.9 54.2 %copy-start.5 = (f32[4096]{0:T(1024)S(1)}, f32[4096]{0:T(1024)}, u32[]{:S(2)}) copy-start(f32[4096]{0:T(1024)} %param.13) | copy-start | bytes 49156
  72.4 158.3 %all-reduce.12.cloned.1.call-start = ((), (), s32[]{:S(2)}) async-start(), calls=%async_computation.2 | async-start | bytes 1048576
  128.3 2.7 copy-start.1
  138.3 9.3 %copy-start.6 = (s32[1,128]{1,0:T(1,128)S(1)}, s32[1,128]{1,0:T(1,128)}, u32[]{:S(2)}) copy-start(s32[1,128]{1,0:T(1,128)} %param.8) | copy-start | bytes 1540
  147.6 10.2 %copy-start.10 = (u32[32]{0:T(128)S(1)}, u32[32]{0:T(128)}, u32[]{:S(2)}) copy-start(u32[32]{0:T(128)} %constant.30) | copy-start | bytes 388
  147.6 84.8 %copy-start.7 = (f32[1,128]{1,0:T(1,128)S(1)}, f32[1,128]{1,0:T(1,128)}, u32[]{:S(2)}) copy-start(f32[1,128]{1,0:T(1,128)} %param.12) | copy-start | bytes 1540
  157.7 231.0 %all-reduce.10.cloned.1.call-start = ((), (), s32[]{:S(2)}) async-start(), calls=%async_computation.1 | async-start | bytes 4194304 | tf_op jit(solution)/shard_map/psum | solution.py:52
  306.6 2.2 copy-start.2
  337.3 177.9 %all-reduce.14.cloned.1.call-start = ((), (), s32[]{:S(2)}) async-start(), calls=%async_computation.3 | async-start | bytes 1048576
  417.1 2.2 copy-start.3
  435.9 81.1 %copy-start.4 = (f32[1,128,128]{2,1,0:T(8,128)S(1)}, f32[1,128,128]{2,1,0:T(8,128)}, u32[]{:S(2)}) copy-start(f32[1,128,128]{2,1,0:T(8,128)} %param.11) | copy-start | bytes 196612
Sparse Core Ops, SparseCore 0:
  72.5 52.4 all-reduce.7
  157.9 72.8 all-reduce.11
  337.5 51.2 all-reduce.9
  446.1 69.1 all-reduce.13
where the time goes:
time: 574 us; the launch traced here: 567 us
  waiting for transfers between devices  224 us (39%)
  blocking collectives  186 us (32%)
  matrix products  73.9 us (13%)
  local copies, waits for them, and re-layouts  54.4 us (9%)
  between operations  14.4 us (3%)
  other arithmetic  13.9 us (2%)
    unnamed x6, waiting for transfers between devices  120 us
    psum x2, waiting for transfers between devices, steepest_of(): summed = lax.psum(adjoint(residual), 'tm')  104 us
    psum x2, blocking collectives, shards(): lax.psum((jnp.sum(image * image, axis=0), jnp.sum(residual * image, axis=...  78.9 us
    all_gather x2, blocking collectives, adjoint(): gathered = lax.all_gather(sent, 'src', axis=0, tiled=True)  64.5 us
    psum x2, blocking collectives, steepest_of(): gamma_now = lax.psum(jnp.sum(steepest * steepest, axis=0), 'src')  43 us
    dot_general x2, matrix products, adjoint(): jnp.dot(spread_cols, products, precision=HIGH).reshape(sources, datasets)  22.4 us
    dot_general x2, matrix products, shards(): jnp.dot(spread_rows, forward_products, precision=HIGH)  20.2 us
    dot_general x2, local copies, waits for them, and re-layouts, adjoint(): jnp.einsum('kac,kar->kcr', blocks, picked.reshape(slot_count, block_size,...  18.7 us
  transfers between devices with their start and end apart: 4, of which 4 were waited for; matrix products, arithmetic and copies ran while one was open for 0% of the time, Pallas kernels for 0%

commit v1 on v0

v1 whole, which is shorter than its diff:
```python
import jax
import jax.numpy as jnp
from jax import lax
from jax.experimental import pallas as pl
from jax.experimental.pallas import tpu as pltpu
from jax.sharding import PartitionSpec as P


ITERS = 2
EPSILON = 1e-06
PARTS = 2
BF = jnp.bfloat16
F32 = jnp.float32


def params(mib):
    return pltpu.CompilerParams(vmem_limit_bytes=mib << 20)


def sds(shape, dtype=F32):
    return jax.ShapeDtypeStruct(shape, dtype)


def xor_permute(array, axis, count, bit):
    return lax.ppermute(array, axis, [(i, i ^ bit) for i in range(count)])


def shards(green, block_rows, block_cols, block_live, data, row_weight, source_gain):
    blocks = green[0]
    slot_count, bs, _ = blocks.shape
    own_rows, ds = data.shape[1], data.shape[2]
    groups = lax.axis_size("src")
    windows = lax.axis_size("tm")
    devices = groups * windows
    sources = source_gain.shape[0]
    wrows = own_rows * groups
    row_blocks = wrows // bs
    col_blocks = sources // bs
    share = sources // windows
    share_blocks = share // bs
    total_rows = wrows * windows
    pairs = windows // 2

    def where():
        tm_index = lax.axis_index("tm")
        return [tm_index & 1, 1 - (tm_index & 1), tm_index >> 1, lax.axis_index("src")]

    gain_rows = source_gain.reshape(windows, 1, share)
    vmem = pl.BlockSpec(memory_space=pltpu.VMEM)
    hbm = pl.BlockSpec(memory_space=pltpu.HBM)

    def kernel(body, out_shape, count, placed=False, in_specs=None, scratch=(), mib=12, cost=None,
               aliases=None):
        def run(*refs):
            body(where(), *refs)

        return pl.pallas_call(
            run if placed else body,
            out_shape=out_shape,
            in_specs=[vmem] * count if in_specs is None else in_specs,
            out_specs=jax.tree.map(lambda _: vmem, out_shape),
            scratch_shapes=scratch,
            input_output_aliases=aliases or {},
            compiler_params=params(mib),
            cost_estimate=cost,
        )

    def after(array, *others):
        return lax.optimization_barrier((array, *others))[0]

    def cost_of(flops, nbytes):
        return pl.CostEstimate(flops=flops, transcendentals=0, bytes_accessed=nbytes)

    def repeat(tile, out_ref, count):
        height = tile.shape[0]
        for b in range(count):
            out_ref[b * height:(b + 1) * height, :] = tile

    def pre_body(data_hbm, w_hbm, sent_ref, r_ref, data_ref, w_ref, sem):
        copies = [
            pltpu.make_async_copy(data_hbm, data_ref, sem.at[0]),
            pltpu.make_async_copy(w_hbm, w_ref, sem.at[1]),
        ]
        for copy in copies:
            copy.start()
        for copy in copies:
            copy.wait()
        residual = w_ref[...] * jnp.transpose(data_ref[...])
        sent_ref[...] = (w_ref[...] * residual).astype(BF)
        r_ref[...] = jnp.transpose(residual)

    sent, residual0 = kernel(
        pre_body, (sds((ds, own_rows), BF), sds((own_rows, ds))), 2, in_specs=[hbm, hbm],
        scratch=[
            pltpu.VMEM((own_rows, ds), F32), pltpu.VMEM((1, own_rows), F32),
            pltpu.SemaphoreType.DMA((2,)),
        ],
    )(*[pltpu.with_memory_space_constraint(x, pltpu.HBM) for x in (data[0], row_weight)])

    own_blocks = own_rows // bs

    def place(device):
        return (device & 1) * (groups // 2) + (device >> 1)

    def split(x, size):
        assert size & (size - 1) == 0
        return x >> (size.bit_length() - 1), x & (size - 1)

    cells = row_blocks * col_blocks
    fetches = 8
    batch = slot_count // fetches

    def build():
        def body(rows_hbm, cols_hbm, live_hbm, blocks_hbm, _, out_ref, rows_ref, cols_ref, live_ref,
                 seen_ref, held_ref, acc_ref, small_sem, sem):
            small = [
                pltpu.make_async_copy(rows_hbm, rows_ref, small_sem.at[0]),
                pltpu.make_async_copy(cols_hbm, cols_ref, small_sem.at[1]),
                pltpu.make_async_copy(live_hbm, live_ref, small_sem.at[2]),
            ]
            copies = [
                pltpu.make_async_copy(
                    blocks_hbm.at[pl.ds(f * batch, batch)], held_ref.at[pl.ds(f * batch, batch)], sem.at[f]
                )
                for f in range(fetches)
            ]
            for copy in small + copies:
                copy.start()

            def clear(i, carry):
                for j in range(col_blocks):
                    seen_ref[i * col_blocks + j] = -1
                return carry

            lax.fori_loop(0, row_blocks, clear, 0)
            for copy in small:
                copy.wait()

            def add(k, carry):
                row = rows_ref[0, k]
                col = cols_ref[0, k]
                cell = row * col_blocks + col
                device, inner = split(row, own_blocks)
                at = pl.multiple_of((place(device) * own_blocks + inner) * bs, bs)
                q, b = split(col, share_blocks)
                lane = pl.multiple_of(b * bs, bs)

                @pl.when(live_ref[0, k] == 1)
                def _():
                    seen = seen_ref[cell]

                    @pl.when(seen == -1)
                    def _():
                        seen_ref[cell] = -2
                        out_ref[q, pl.ds(at, bs), pl.ds(lane, bs)] = held_ref[k]

                    @pl.when(seen == -2)
                    def _():
                        seen_ref[cell] = k
                        total = out_ref[q, pl.ds(at, bs), pl.ds(lane, bs)].astype(F32) + held_ref[k].astype(F32)
                        acc_ref[k] = total
                        out_ref[q, pl.ds(at, bs), pl.ds(lane, bs)] = total.astype(BF)

                    @pl.when(seen >= 0)
                    def _():
                        total = acc_ref[seen] + held_ref[k].astype(F32)
                        acc_ref[seen] = total
                        out_ref[q, pl.ds(at, bs), pl.ds(lane, bs)] = total.astype(BF)

                return carry

            for f in range(fetches):
                copies[f].wait()
                lax.fori_loop(f * batch, (f + 1) * batch, add, 0, unroll=4)

        def clear_body(out_ref):
            def clear(i, carry):
                at = pl.multiple_of(i * bs, bs)
                for q in range(windows):
                    out_ref[q, pl.ds(at, bs), :] = jnp.zeros((bs, share), BF)
                return carry

            lax.fori_loop(0, row_blocks, clear, 0)

        empty = kernel(
            clear_body, pltpu.VMEM((windows, wrows, share), BF), 0, in_specs=[],
            cost=cost_of(0, wrows * sources * 2),
        )()
        empty = pltpu.with_memory_space_constraint(empty, pltpu.VMEM)
        built = kernel(
            body, pltpu.VMEM((windows, wrows, share), BF), 5, in_specs=[hbm] * 4 + [vmem], aliases={4: 0},
            scratch=[pltpu.SMEM((1, slot_count), jnp.int32)] * 3 + [
                pltpu.SMEM((cells,), jnp.int32),
                pltpu.VMEM((slot_count, bs, bs), BF),
                pltpu.VMEM((slot_count, bs, bs), F32),
                pltpu.SemaphoreType.DMA((3,)),
                pltpu.SemaphoreType.DMA((fetches,)),
            ],
            cost=cost_of(0, wrows * sources * 6),
        )(
            *[
                pltpu.with_memory_space_constraint(x, pltpu.HBM)
                for x in (block_rows, block_cols, block_live, blocks)
            ],
            empty,
        )
        return pltpu.with_memory_space_constraint(built, pltpu.VMEM)

    def gather(piece, last=None):
        held = {0: piece}
        held[1] = xor_permute(piece, "src", groups, 1)
        for k in range(2, groups, 2):
            held[k] = xor_permute(piece, "src", groups, k)
        for k in range(2, groups, 2):
            held[k + 1] = xor_permute(held[k], "src", groups, 1)
        if last is not None:
            for k in range(3, groups, 2):
                held[k] = after(held[k], last)

        def body(here, *refs):
            for k in range(groups):
                at = pl.multiple_of(place(here[3] ^ k) * own_rows, own_rows)
                refs[-1][:, pl.ds(at, own_rows)] = refs[k][...]

        return kernel(body, sds((ds, wrows), BF), groups, placed=True)(
            *[held[k] for k in range(groups)]
        )

    width = share // PARTS
    chunks = [(i, slice(h * width, (h + 1) * width)) for i in range(pairs) for h in range(PARTS)]
    last = len(chunks) - 1
    quarter = cost_of(2 * ds * wrows * share, wrows * share * 2)

    def adjoint_part(sent, chunk, parity, arrived=None):
        index, lanes = chunk

        def body(here, z_ref, g_ref, *refs):
            product = jnp.dot(
                z_ref[...], g_ref[2 * index + here[parity], :, lanes], preferred_element_type=F32
            )
            if arrived is None:
                refs[0][...] = product.astype(BF)
            else:
                product = product + refs[0][...].astype(F32)
                refs[1][...] = product.astype(BF)
                refs[2][...] = product

        more = () if arrived is None else (arrived,)
        shape = sds((ds, width), BF)
        return kernel(
            body, (shape, sds((ds, width))) if more else shape,
            2 + len(more), placed=True, cost=quarter,
        )(sent, matrix, *more)

    def adjoint(sent):
        away, arrived, mine, theirs = [], [], [], []

        def ahead(j):
            z = sent if j < 2 else after(sent, mine[j - 2])
            away.append(adjoint_part(z, chunks[j], 1))
            arrived.append(xor_permute(away[j], "tm", windows, 1))

        ahead(0)
        for j in range(last + 1):
            if j < last:
                ahead(j + 1)
            total, own = adjoint_part(sent, chunks[j], 0, after(arrived[j], away[-1]))
            bit = 2
            while bit * 2 < windows:
                total, own = add(own, xor_permute(total, "tm", windows, bit))
                bit *= 2
            mine.append(own)
            theirs.append(xor_permute(total, "tm", windows, bit))
        return mine, theirs

    def add(a, b):
        def body(a_ref, b_ref, sent_ref, own_ref):
            total = a_ref[...] + b_ref[...].astype(F32)
            sent_ref[...] = total.astype(BF)
            own_ref[...] = total

        return kernel(body, (sds((ds, width), BF), sds((ds, width))), 2)(a, b)

    def scale(a, b, chunk):
        index, lanes = chunk

        def body(here, a_ref, b_ref, gain_ref, out_ref):
            gain = gain_ref[2 * index + here[0], :, lanes]
            total = a_ref[...] + b_ref[...].astype(F32)
            out_ref[...] = (gain * (gain * total)).astype(BF)

        return kernel(body, sds((ds, width), BF), 3, placed=True)(a, b, gain_rows)

    def own_share(mine, theirs):
        count = len(chunks)

        def body(here, *refs):
            gain_ref, s_ref, gamma_ref = refs[2 * count:]
            for i in range(pairs):

                @pl.when(here[2] == i)
                def _():
                    gamma = jnp.zeros((1, ds), F32)
                    for h in range(PARTS):
                        lanes = slice(h * width, (h + 1) * width)
                        j = i * PARTS + h
                        total = refs[j][...] + refs[count + j][...].astype(F32)
                        steepest = jnp.transpose(gain_ref[2 * i + here[0], :, lanes] * total)
                        s_ref[lanes, :] = steepest
                        gamma = gamma + rows_sum(steepest * steepest)
                    gamma_ref[...] = jnp.broadcast_to(gamma, (8, ds))

        return kernel(body, (sds((share, ds)), sds((8, ds))), 2 * count + 1, placed=True)(*mine, *theirs, gain_rows)

    half_rows = wrows // 2

    def forward_part(scaled, chunk, parities, before=None):
        index, lanes = chunk

        def body(here, g_ref, *refs):
            total = None
            for s_ref, parity in zip(refs, parities):
                product = lax.dot_general(
                    s_ref[...], g_ref[2 * index + here[parity], :, lanes], (((1,), (1,)), ((), ())),
                    preferred_element_type=F32,
                )
                total = product if total is None else total + product
            if before is not None:
                total = total + refs[len(parities)][...]
            refs[-1][...] = total

        more = () if before is None else (before,)
        return kernel(
            body, sds((ds, wrows)), 1 + len(scaled) + len(more), placed=True, cost=quarter
        )(matrix, *scaled, *more)

    steps = groups // 2
    near = steps // 2
    part_rows = half_rows // 2

    def forward_last(scaled, chunk, before, dtype):
        index, lanes = chunk

        def body(here, g_ref, s_ref, before_ref, far_ref, near_ref, keep_ref):
            own = here[3] & 1
            group = (here[3] >> 1) // near if near > 1 else here[3] >> 1
            away = (1 - own) * half_rows
            for at, out_ref in (
                (away + (1 - group) * part_rows, far_ref),
                (away + group * part_rows, near_ref),
                (own * half_rows, keep_ref),
            ):
                rows = pl.ds(pl.multiple_of(at, own_rows), out_ref.shape[1])
                product = lax.dot_general(
                    s_ref[...], g_ref[2 * index + here[1], rows, lanes], (((1,), (1,)), ((), ())),
                    preferred_element_type=F32,
                )
                out_ref[...] = (product + before_ref[:, rows]).astype(out_ref.dtype)

        return kernel(
            body,
            (sds((ds, part_rows), dtype), sds((ds, part_rows), dtype), sds((ds, half_rows))),
            3, placed=True, cost=quarter,
        )(matrix, scaled, before)

    def pair_sums(arrived, keep, dtype, ks):
        def body(here, arrived_ref, keep_ref, *out_refs):
            for k, out_ref in zip(ks, out_refs):
                block = (here[3] >> 1) ^ k
                inner = pl.multiple_of((block & (near - 1)) * own_rows, own_rows)
                at = pl.multiple_of(block * own_rows, own_rows)
                total = keep_ref[:, pl.ds(at, own_rows)] + arrived_ref[:, pl.ds(inner, own_rows)].astype(F32)
                out_ref[...] = total.astype(out_ref.dtype)

        return kernel(body, tuple(sds((ds, own_rows), dtype if k else F32) for k in ks), 2, placed=True)(arrived, keep)

    def scatter(far, close, keep, dtype, beside):
        far = xor_permute(far, "src", groups, 1)
        close = xor_permute(close, "src", groups, 1)
        sums = list(pair_sums(after(far, beside), keep, dtype, range(near, steps)))
        sums = [xor_permute(x, "src", groups, 2 * k) for k, x in zip(range(near, steps), sums)]
        mine = list(pair_sums(close, keep, dtype, range(near)))
        return mine[:1] + [xor_permute(x, "src", groups, 2 * k) for k, x in zip(range(1, near), mine[1:])] + sums

    def forward(mine, theirs, out):
        total = None
        for j in range(last + 1):
            scaled = scale(mine[j], after(theirs[j], mine[-1]), chunks[j])
            other = xor_permute(scaled, "tm", windows, 1)
            if j < last:
                total = forward_part([scaled, other], chunks[j], [0, 1], total)
            else:
                total = forward_part([scaled], chunks[j], [0], total)
                far, close, keep = forward_last(other, chunks[j], total, out)
        steepest, gamma = own_share(mine[:-1] + [after(mine[-1], far)], theirs)
        return steepest, gamma, scatter(far, close, keep, out, gamma)

    def rows_sum(x):
        return jnp.sum(x, axis=0, keepdims=True)

    def sum_blocks(ref, height, count):
        total = ref[0:height, :].astype(F32)
        for b in range(1, count):
            total = total + ref[b * height:(b + 1) * height, :].astype(F32)
        return total

    parts = groups // 2

    def sum_parts(refs):
        total = refs[0][...]
        for ref in refs[1:]:
            total = total + ref[...].astype(F32)
        return total

    def first_norm_body(*refs):
        w_ref, gamma_ref, q_ref, scal_ref = refs[parts:]
        image = jnp.transpose(w_ref[...] * sum_parts(refs[:parts]))
        q_ref[...] = image
        zero = jnp.zeros((6, ds), F32)
        tile = jnp.concatenate([gamma_ref[0:1, :], rows_sum(image * image), zero], axis=0)
        repeat(tile, scal_ref, devices)

    def first_step_body(scal_ref, q_ref, r_ref, w_ref, sent_ref, r_out, keep_ref):
        tile = sum_blocks(scal_ref, 8, devices)
        keep_ref[...] = tile
        step = tile[0:1, :] / (tile[1:2, :] + EPSILON)
        residual = r_ref[...] - step * q_ref[...]
        r_out[...] = residual
        sent_ref[...] = (w_ref[...] * jnp.transpose(residual)).astype(BF)

    def last_norm_body(*refs):
        w_ref, gamma_ref, q_ref, r_ref, a_ref, scal_ref = refs[parts:]
        image = jnp.transpose(w_ref[...] * sum_parts(refs[:parts]))
        a_ref[...] = image
        before, residual = q_ref[...], r_ref[...]
        rows = [
            gamma_ref[0:1, :],
            rows_sum(image * image),
            rows_sum(image * before),
            rows_sum(image * residual),
            rows_sum(before * residual),
            rows_sum(residual * residual),
            jnp.zeros((2, ds), F32),
        ]
        repeat(jnp.concatenate(rows, axis=0), scal_ref, devices)

    def last_step_body(scal_ref, keep_ref, q_ref, a_ref, r_ref, s0_ref, s1_ref, x_ref, r_out, m_ref):
        tile = sum_blocks(scal_ref, 8, devices)
        gamma, norm = keep_ref[0:1, :], keep_ref[1:2, :]
        step = gamma / (norm + EPSILON)
        gamma_next = tile[0:1, :]
        beta = gamma_next / (gamma + EPSILON)
        image_norm = tile[1:2, :] + 2.0 * beta * tile[2:3, :] + beta * beta * norm
        step_next = gamma_next / (image_norm + EPSILON)
        cross = tile[3:4, :] + beta * tile[4:5, :]
        square = tile[5:6, :]
        m_ref[0:1, :] = square / total_rows
        m_ref[1:2, :] = (
            square - 2.0 * step_next * cross + step_next * step_next * image_norm
        ) / total_rows
        r_out[...] = r_ref[...] - step_next * (a_ref[...] + beta * q_ref[...])
        x_ref[...] = (step + step_next * beta) * s0_ref[...] + step_next * s1_ref[...]

    def everywhere(tile):
        return lax.all_to_all(tile, ("src", "tm"), 0, 0, tiled=True)

    square_sds = sds((own_rows, ds))
    scal_sds = sds((devices * 8, ds))
    matrix = build()
    mine, theirs = adjoint(gather(sent, matrix))
    steepest0, gamma0, image = forward(mine, theirs, F32)
    image0, sums = kernel(first_norm_body, (square_sds, scal_sds), parts + 2)(*image, row_weight, gamma0)
    sums = everywhere(sums)
    sent, residual1, kept = kernel(
        first_step_body, (sds((ds, own_rows), BF), square_sds, sds((8, ds))), 4
    )(sums, image0, residual0, row_weight)
    mine, theirs = adjoint(gather(sent))
    steepest1, gamma1, image = forward(mine, theirs, F32)
    image1, sums = kernel(
        last_norm_body, (square_sds, scal_sds), parts + 4
    )(*image, row_weight, gamma1, image0, residual1)
    sums = everywhere(sums)
    solved, residual, misfit = kernel(
        last_step_body, (sds((share, ds)), square_sds, sds((ITERS, ds))), 7
    )(sums, kept, image0, image1, residual1, steepest0, steepest1)
    return solved, residual[None], misfit


def solution(mesh):
    placed = (
        P("tm", "src", None, None),
        P("tm", "src"),
        P("tm", "src"),
        P("tm", "src"),
        P("tm", "src", None),
        P("tm", "src"),
        P("src"),
    )
    return jax.shard_map(
        shards,
        mesh=mesh,
        in_specs=placed,
        out_specs=(P(("src", "tm"), None), P("tm", "src", None), P()),
        check_vma=False,
    )
```

time: 574 us -> 127 us (0.22); the launches traced: 567 us -> 127 us
  waiting for transfers between devices: 224 us -> 41.5 us
  blocking collectives: 186 us -> 21.9 us
  matrix products: 73.9 us -> 0 us
  local copies, waits for them, and re-layouts: 54.4 us -> 0.01 us
  starting transfers between devices: 0.34 us -> 41 us
  Pallas kernels: 0 us -> 21.3 us
  other arithmetic: 13.9 us -> 0 us
  between operations: 14.4 us -> 1.17 us
    psum x4 -> x0, blocking collectives: 122 us -> none  [the longest x2 78.9 us: shards(): lax.psum((jnp.sum(image * image, axis=0), jnp.sum(residual * image, axis=...]
    unnamed x6 -> x0, waiting for transfers between devices: 120 us -> none
    psum x2 -> x0, waiting for transfers between devices: 104 us -> none  [steepest_of(): summed = lax.psum(adjoint(residual), 'tm')]
    dot_general x12 -> x0, matrix products: 73.9 us -> none  [the longest x2 22.4 us: adjoint(): jnp.dot(spread_cols, products, precision=HIGH).reshape(sources, datasets)]
    all_gather x2 -> x0, blocking collectives: 64.5 us -> none  [adjoint(): gathered = lax.all_gather(sent, 'src', axis=0, tiled=True)]
    ppermute x0 -> x48, waiting for transfers between devices: none -> 41.5 us  [xor_permute(): return lax.ppermute(array, axis, [(i, i ^ bit) for i in range(count)])]
    ppermute x0 -> x48, starting transfers between devices: none -> 41 us  [xor_permute(): return lax.ppermute(array, axis, [(i, i ^ bit) for i in range(count)])]
    dot_general x4 -> x0, local copies, waits for them, and re-layouts: 37.4 us -> none  [the longest x2 18.7 us: adjoint(): jnp.einsum('kac,kar->kcr', blocks, picked.reshape(slot_count, block_size,...]
  transfers between devices with their start and end apart: 4 -> 48, of which waited for: 4 -> 25; matrix products, arithmetic and copies ran while one was open for 0% -> 0% of each run, Pallas kernels for 0% -> 14%
where the time goes in v1:
time: 127 us
  waiting for transfers between devices  41.5 us (33%)
  starting transfers between devices  41 us (32%)
  blocking collectives  21.9 us (17%)
  Pallas kernels  21.3 us (17%)
    ppermute x48, waiting for transfers between devices, xor_permute(): return lax.ppermute(array, axis, [(i, i ^ bit) for i in range(count)])  41.5 us
    ppermute x48, starting transfers between devices, xor_permute(): return lax.ppermute(array, axis, [(i, i ^ bit) for i in range(count)])  41 us
    all_to_all x2, blocking collectives, everywhere(): return lax.all_to_all(tile, ('src', 'tm'), 0, 0, tiled=True)  21.9 us
    pallas_call x8, Pallas kernels, forward_part(): kernel(body, sds((ds, wrows)), 1 + len(scaled) + len(more), placed=True,...  5.92 us
    pallas_call x1, Pallas kernels, build(): kernel(body, pltpu.VMEM((windows, wrows, share), BF), 5, in_specs=[hbm] *...  5.28 us
    pallas_call x16, Pallas kernels, adjoint_part(): kernel(body, (shape, sds((ds, width))) if more else shape, 2 + len(more),...  5.13 us
  transfers between devices with their start and end apart: 48, of which 25 were waited for; matrix products, arithmetic and copies ran while one was open for 0% of the time, Pallas kernels for 14%

profile of v1, /device:TPU:0, one launch (start us, length us, event | category | flops | bytes accessed | tf_op | source)
XLA Modules:
  0.0 127.0 jit_solution(17652867071699062777)
XLA Ops:
  0.6 1.0 shard_map.96
  1.7 3.1 %collective-permute-start.1 = (bf16[128,128]{1,0:T(8,128)(2,1)S(1)}, bf16[128,128]{1,0:T(8,128)(2,1)S(1)}, u32[]{:S(2)}, u32[]{:S(2)}) collective-permute-start(bf16[128,128]{1,0:T(8,128)(2,1)S(1)} %get-tuple-element.76.refs_0_), channel_id=1, source_target_pairs={{0,8},{4,12},{8,0},{12,4},{16,24},{20,28},{24,16},{28,20},{1,9},{5... | collective-permute-start | bytes 98312 | tf_op jit(solution)/shard_map/ppermute | solution.py:25
  4.8 2.6 %collective-permute-start.3 = (bf16[128,128]{1,0:T(8,128)(2,1)S(1)}, bf16[128,128]{1,0:T(8,128)(2,1)S(1)}, u32[]{:S(2)}, u32[]{:S(2)}) collective-permute-start(bf16[128,128]{1,0:T(8,128)(2,1)S(1)} %get-tuple-element.76.refs_0_), channel_id=1, source_target_pairs={{0,16},{4,20},{8,24},{12,28},{16,0},{20,4},{24,8},{28,12},{1,17},{... | collective-permute-start | bytes 98312 | tf_op jit(solution)/shard_map/ppermute | solution.py:25
  7.4 1.7 %collective-permute-start.2 = (bf16[128,128]{1,0:T(8,128)(2,1)S(1)}, bf16[128,128]{1,0:T(8,128)(2,1)S(1)}, u32[]{:S(2)}, u32[]{:S(2)}) collective-permute-start(bf16[128,128]{1,0:T(8,128)(2,1)S(1)} %collective-permute-done.1.refs_2_), channel_id=1, source_target_pairs={{0,4},{4,0},{8,12},{12,8},{16,20},{20,16},{24,28},{28,24},{1,5},{5... | collective-permute-start | bytes 98312 | tf_op jit(solution)/shard_map/ppermute | solution.py:25
  9.1 1.1 collective-permute-done.3.refs_4_
  10.2 1.5 %collective-permute-start.4 = (bf16[128,128]{1,0:T(8,128)(2,1)S(1)}, bf16[128,128]{1,0:T(8,128)(2,1)S(1)}, u32[]{:S(2)}, u32[]{:S(2)}) collective-permute-start(bf16[128,128]{1,0:T(8,128)(2,1)S(1)} %collective-permute-done.3.refs_4_), channel_id=1, source_target_pairs={{0,4},{4,0},{8,12},{12,8},{16,20},{20,16},{24,28},{28,24},{1,5},{5... | collective-permute-start | bytes 98312 | tf_op jit(solution)/shard_map/ppermute | solution.py:25
  11.7 1.4 %collective-permute-done.5.refs_6_ = bf16[128,128]{1,0:T(8,128)(2,1)S(1)} collective-permute-done((bf16[128,128]{1,0:T(8,128)(2,1)S(1)}, bf16[128,128]{1,0:T(8,128)(2,1)S(1)}, u32[]{:S(2)}, u32[]{:S(2)}) %collective-permute-start.5) | collective-permute-done | bytes 32800 | tf_op jit(solution)/shard_map/ppermute | solution.py:25
  13.1 1.5 %collective-permute-start.6 = (bf16[128,128]{1,0:T(8,128)(2,1)S(1)}, bf16[128,128]{1,0:T(8,128)(2,1)S(1)}, u32[]{:S(2)}, u32[]{:S(2)}) collective-permute-start(bf16[128,128]{1,0:T(8,128)(2,1)S(1)} %collective-permute-done.5.refs_6_), channel_id=1, source_target_pairs={{0,4},{4,0},{8,12},{12,8},{16,20},{20,16},{24,28},{28,24},{1,5},{5... | collective-permute-start | bytes 98312 | tf_op jit(solution)/shard_map/ppermute | solution.py:25
  14.6 0.5 collective-permute-start
  15.1 0.6 shard_map.94._
  15.7 5.3 %shard_map.95.refs_1_.refs_0_ = bf16[4,1024,1024]{2,1,0:T(8,128)(2,1)S(1)} custom-call(s32[1,128]{1,0:T(1,128)} %rows_hbm.1, s32[1,128]{1,0:T(1,128)} %cols_hbm.1, s32[1,128]{1,0:T(1,128)} %live_hbm.1, bf16[128,128,128]{2,1,0:T(8,128)(2,1)} %bitcast.22, bf16[4,1024,1024]{2,1,0:T(8,128)(2,1)S(1)} %shard_map.94._), custom_call_target="tpu_custom_call", output_to_operand_aliasing={{}: (4, {})} | custom-call | bytes 25165824 | tf_op jit(solution)/shard_map/pallas_call | solution.py:190
  21.8 0.6 collective-permute-start.7
  24.8 2.0 %collective-permute-start.15 = (bf16[128,512]{1,0:T(8,128)(2,1)S(1)}, bf16[128,512]{1,0:T(8,128)(2,1)S(1)}, u32[]{:S(2)}, u32[]{:S(2)}) collective-permute-start(bf16[128,512]{1,0:T(8,128)(2,1)S(1)} %get-tuple-element.94), channel_id=1, source_target_pairs={{0,2},{1,3},{2,0},{3,1},{4,6},{5,7},{6,4},{7,5},{8,10},{9,11},{10,... | collective-permute-start | bytes 393224 | tf_op jit(solution)/shard_map/ppermute | solution.py:25
  27.6 2.1 %collective-permute-start.10 = (bf16[128,512]{1,0:T(8,128)(2,1)S(1)}, bf16[128,512]{1,0:T(8,128)(2,1)S(1)}, u32[]{:S(2)}, u32[]{:S(2)}) collective-permute-start(bf16[128,512]{1,0:T(8,128)(2,1)S(1)} %get-tuple-element.88), channel_id=1, source_target_pairs={{0,2},{1,3},{2,0},{3,1},{4,6},{5,7},{6,4},{7,5},{8,10},{9,11},{10,... | collective-permute-start | bytes 393224 | tf_op jit(solution)/shard_map/ppermute | solution.py:25
  29.6 1.5 %collective-permute-done.17.refs_1_.refs_4_ = bf16[128,512]{1,0:T(8,128)(2,1)S(1)} collective-permute-done((bf16[128,512]{1,0:T(8,128)(2,1)S(1)}, bf16[128,512]{1,0:T(8,128)(2,1)S(1)}, u32[]{:S(2)}, u32[]{:S(2)}) %collective-permute-start.17) | collective-permute-done | bytes 131104 | tf_op jit(solution)/shard_map/ppermute | solution.py:25
  31.3 2.7 %collective-permute-done.15.refs_1_.refs_5_ = bf16[128,512]{1,0:T(8,128)(2,1)S(1)} collective-permute-done((bf16[128,512]{1,0:T(8,128)(2,1)S(1)}, bf16[128,512]{1,0:T(8,128)(2,1)S(1)}, u32[]{:S(2)}, u32[]{:S(2)}) %collective-permute-start.15) | collective-permute-done | bytes 131104 | tf_op jit(solution)/shard_map/ppermute | solution.py:25
  34.1 2.7 %collective-permute-done.13.refs_1_.refs_6_ = bf16[128,512]{1,0:T(8,128)(2,1)S(1)} collective-permute-done((bf16[128,512]{1,0:T(8,128)(2,1)S(1)}, bf16[128,512]{1,0:T(8,128)(2,1)S(1)}, u32[]{:S(2)}, u32[]{:S(2)}) %collective-permute-start.13) | collective-permute-done | bytes 131104 | tf_op jit(solution)/shard_map/ppermute | solution.py:25
  36.9 1.9 %collective-permute-done.10.refs_1_.refs_7_ = bf16[128,512]{1,0:T(8,128)(2,1)S(1)} collective-permute-done((bf16[128,512]{1,0:T(8,128)(2,1)S(1)}, bf16[128,512]{1,0:T(8,128)(2,1)S(1)}, u32[]{:S(2)}, u32[]{:S(2)}) %collective-permute-start.10) | collective-permute-done | bytes 131104 | tf_op jit(solution)/shard_map/ppermute | solution.py:25
  38.9 0.8 shard_map.110.refs_3_
  39.7 0.8 shard_map.111.refs_3_
  40.6 0.8 shard_map.112.refs_2_
  41.9 0.5 shard_map.114
  42.8 1.7 %collective-permute-start.19 = (f32[128,256]{1,0:T(8,128)S(1)}, f32[128,256]{1,0:T(8,128)S(1)}, u32[]{:S(2)}, u32[]{:S(2)}) collective-permute-start(f32[128,256]{1,0:T(8,128)S(1)} %get-tuple-element.98), channel_id=1, source_target_pairs={{0,4},{4,0},{8,12},{12,8},{16,20},{20,16},{24,28},{28,24},{1,5},{5... | collective-permute-start | bytes 393224 | tf_op jit(solution)/shard_map/ppermute | solution.py:25
  44.8 4.1 %collective-permute-done.21.refs_0_ = f32[128,256]{1,0:T(8,128)S(1)} collective-permute-done((f32[128,256]{1,0:T(8,128)S(1)}, f32[128,256]{1,0:T(8,128)S(1)}, u32[]{:S(2)}, u32[]{:S(2)}) %collective-permute-start.21) | collective-permute-done | bytes 131104 | tf_op jit(solution)/shard_map/ppermute | solution.py:25
  48.9 0.5 collective-permute-start.22
  49.4 1.0 collective-permute-start.23
  50.4 0.8 collective-permute-done.19.refs_0_
  51.2 1.3 %collective-permute-start.20 = (f32[128,128]{1,0:T(8,128)S(1)}, f32[128,128]{1,0:T(8,128)S(1)}, u32[]{:S(2)}, u32[]{:S(2)}) collective-permute-start(f32[128,128]{1,0:T(8,128)S(1)} %get-tuple-element.101), channel_id=1, source_target_pairs={{0,8},{4,12},{8,0},{12,4},{16,24},{20,28},{24,16},{28,20},{1,9},{5... | collective-permute-start | bytes 196616 | tf_op jit(solution)/shard_map/ppermute | solution.py:25
  52.6 2.3 %collective-permute-done.22.refs_2_ = f32[128,128]{1,0:T(8,128)S(1)} collective-permute-done((f32[128,128]{1,0:T(8,128)S(1)}, f32[128,128]{1,0:T(8,128)S(1)}, u32[]{:S(2)}, u32[]{:S(2)}) %collective-permute-start.22) | collective-permute-done | bytes 65568 | tf_op jit(solution)/shard_map/ppermute | solution.py:25
  54.9 0.7 collective-permute-done.23.refs_3_
  55.6 0.9 collective-permute-done.20.refs_1_
  56.7 10.8 %all_to_all.22 = f32[32,8,128]{2,1,0:T(8,128)S(1)} all-to-all(f32[32,8,128]{2,1,0:T(8,128)S(1)} %bitcast.20), channel_id=1, replica_groups=mesh['src'=8,'tm'=4] {'src','tm'}, dimensions={0} | all-to-all | bytes 262144 | tf_op jit(solution)/shard_map/all_to_all | solution.py:465
  67.6 0.7 collective-permute-start.25
  68.4 1.2 collective-permute-start.27
  69.6 2.5 %collective-permute-start.29 = (bf16[128,128]{1,0:T(8,128)(2,1)S(1)}, bf16[128,128]{1,0:T(8,128)(2,1)S(1)}, u32[]{:S(2)}, u32[]{:S(2)}) collective-permute-start(bf16[128,128]{1,0:T(8,128)(2,1)S(1)} %get-tuple-element.111.refs_0_), channel_id=1, source_target_pairs={{0,24},{4,28},{8,16},{12,20},{16,8},{20,12},{24,0},{28,4},{1,25},{... | collective-permute-start | bytes 98312 | tf_op jit(solution)/shard_map/ppermute | solution.py:25
  72.1 0.7 collective-permute-start.24
  72.8 1.4 %collective-permute-start.26 = (bf16[128,128]{1,0:T(8,128)(2,1)S(1)}, bf16[128,128]{1,0:T(8,128)(2,1)S(1)}, u32[]{:S(2)}, u32[]{:S(2)}) collective-permute-start(bf16[128,128]{1,0:T(8,128)(2,1)S(1)} %collective-permute-done.25.refs_2_), channel_id=1, source_target_pairs={{0,4},{4,0},{8,12},{12,8},{16,20},{20,16},{24,28},{28,24},{1,5},{5... | collective-permute-start | bytes 98312 | tf_op jit(solution)/shard_map/ppermute | solution.py:25
  74.1 0.7 collective-permute-start.28
  74.8 0.5 collective-permute-done.29.refs_6_
  75.3 0.8 collective-permute-start.30
  76.4 0.6 collective-permute-done.26.refs_3_
  76.9 1.1 collective-permute-done.28.refs_5_
  78.1 1.2 collective-permute-done.30.refs_7_
  80.1 0.6 collective-permute-start.31
  83.4 1.6 %collective-permute-start.39 = (bf16[128,512]{1,0:T(8,128)(2,1)S(1)}, bf16[128,512]{1,0:T(8,128)(2,1)S(1)}, u32[]{:S(2)}, u32[]{:S(2)}) collective-permute-start(bf16[128,512]{1,0:T(8,128)(2,1)S(1)} %get-tuple-element.126), channel_id=1, source_target_pairs={{0,2},{1,3},{2,0},{3,1},{4,6},{5,7},{6,4},{7,5},{8,10},{9,11},{10,... | collective-permute-start | bytes 393224 | tf_op jit(solution)/shard_map/ppermute | solution.py:25
  86.2 1.7 %collective-permute-start.34 = (bf16[128,512]{1,0:T(8,128)(2,1)S(1)}, bf16[128,512]{1,0:T(8,128)(2,1)S(1)}, u32[]{:S(2)}, u32[]{:S(2)}) collective-permute-start(bf16[128,512]{1,0:T(8,128)(2,1)S(1)} %get-tuple-element.120), channel_id=1, source_target_pairs={{0,2},{1,3},{2,0},{3,1},{4,6},{5,7},{6,4},{7,5},{8,10},{9,11},{10,... | collective-permute-start | bytes 393224 | tf_op jit(solution)/shard_map/ppermute | solution.py:25
  87.9 1.5 %collective-permute-done.41.refs_1_.refs_4_ = bf16[128,512]{1,0:T(8,128)(2,1)S(1)} collective-permute-done((bf16[128,512]{1,0:T(8,128)(2,1)S(1)}, bf16[128,512]{1,0:T(8,128)(2,1)S(1)}, u32[]{:S(2)}, u32[]{:S(2)}) %collective-permute-start.41) | collective-permute-done | bytes 131104 | tf_op jit(solution)/shard_map/ppermute | solution.py:25
  89.5 2.7 %collective-permute-done.39.refs_1_.refs_5_ = bf16[128,512]{1,0:T(8,128)(2,1)S(1)} collective-permute-done((bf16[128,512]{1,0:T(8,128)(2,1)S(1)}, bf16[128,512]{1,0:T(8,128)(2,1)S(1)}, u32[]{:S(2)}, u32[]{:S(2)}) %collective-permute-start.39) | collective-permute-done | bytes 131104 | tf_op jit(solution)/shard_map/ppermute | solution.py:25
  92.3 2.7 %collective-permute-done.37.refs_1_.refs_6_ = bf16[128,512]{1,0:T(8,128)(2,1)S(1)} collective-permute-done((bf16[128,512]{1,0:T(8,128)(2,1)S(1)}, bf16[128,512]{1,0:T(8,128)(2,1)S(1)}, u32[]{:S(2)}, u32[]{:S(2)}) %collective-permute-start.37) | collective-permute-done | bytes 131104 | tf_op jit(solution)/shard_map/ppermute | solution.py:25
  95.1 1.9 %collective-permute-done.34.refs_1_.refs_7_ = bf16[128,512]{1,0:T(8,128)(2,1)S(1)} collective-permute-done((bf16[128,512]{1,0:T(8,128)(2,1)S(1)}, bf16[128,512]{1,0:T(8,128)(2,1)S(1)}, u32[]{:S(2)}, u32[]{:S(2)}) %collective-permute-start.34) | collective-permute-done | bytes 131104 | tf_op jit(solution)/shard_map/ppermute | solution.py:25
  97.1 0.8 shard_map.133.refs_3_
  98.0 0.8 shard_map.134.refs_3_
  98.8 0.8 shard_map.135.refs_2_
  99.6 0.5 shard_map.136.refs_2_
  100.2 0.5 shard_map.137
  100.7 0.9 collective-permute-start.45
  101.6 1.2 collective-permute-start.43
  103.0 4.1 %collective-permute-done.45.refs_0_ = f32[128,256]{1,0:T(8,128)S(1)} collective-permute-done((f32[128,256]{1,0:T(8,128)S(1)}, f32[128,256]{1,0:T(8,128)S(1)}, u32[]{:S(2)}, u32[]{:S(2)}) %collective-permute-start.45) | collective-permute-done | bytes 131104 | tf_op jit(solution)/shard_map/ppermute | solution.py:25
  107.2 2.6 %collective-permute-start.47 = (f32[128,128]{1,0:T(8,128)S(1)}, f32[128,128]{1,0:T(8,128)S(1)}, u32[]{:S(2)}, u32[]{:S(2)}) collective-permute-start(f32[128,128]{1,0:T(8,128)S(1)} %get-tuple-element.139), channel_id=1, source_target_pairs={{0,24},{4,28},{8,16},{12,20},{16,8},{20,12},{24,0},{28,4},{1,25},{... | collective-permute-start | bytes 196616 | tf_op jit(solution)/shard_map/ppermute | solution.py:25
  109.8 1.0 collective-permute-start.44
  110.8 3.5 %collective-permute-done.46.refs_2_ = f32[128,128]{1,0:T(8,128)S(1)} collective-permute-done((f32[128,128]{1,0:T(8,128)S(1)}, f32[128,128]{1,0:T(8,128)S(1)}, u32[]{:S(2)}, u32[]{:S(2)}) %collective-permute-start.46) | collective-permute-done | bytes 65568 | tf_op jit(solution)/shard_map/ppermute | solution.py:25
  114.3 0.5 collective-permute-done.44.refs_1_
  115.0 11.1 %all_to_all.23 = f32[32,8,128]{2,1,0:T(8,128)S(1)} all-to-all(f32[32,8,128]{2,1,0:T(8,128)S(1)} %bitcast.21), channel_id=1, replica_groups=mesh['src'=8,'tm'=4] {'src','tm'}, dimensions={0} | all-to-all | bytes 262144 | tf_op jit(solution)/shard_map/all_to_all | solution.py:465
  126.0 0.9 shard_map.142
  (87 shorter events, 11.6 us)
Async XLA Ops:
  1.7 5.7 %collective-permute-start.1 = (bf16[128,128]{1,0:T(8,128)(2,1)S(1)}, bf16[128,128]{1,0:T(8,128)(2,1)S(1)}, u32[]{:S(2)}, u32[]{:S(2)}) collective-permute-start(bf16[128,128]{1,0:T(8,128)(2,1)S(1)} %get-tuple-element.76.refs_0_), channel_id=1, source_target_pairs={{0,8},{4,12},{8,0},{12,4},{16,24},{20,28},{24,16},{28,20},{1,9},{5... | collective-permute-start | bytes 98312 | tf_op jit(solution)/shard_map/ppermute | solution.py:25
  4.8 5.4 %collective-permute-start.3 = (bf16[128,128]{1,0:T(8,128)(2,1)S(1)}, bf16[128,128]{1,0:T(8,128)(2,1)S(1)}, u32[]{:S(2)}, u32[]{:S(2)}) collective-permute-start(bf16[128,128]{1,0:T(8,128)(2,1)S(1)} %get-tuple-element.76.refs_0_), channel_id=1, source_target_pairs={{0,16},{4,20},{8,24},{12,28},{16,0},{20,4},{24,8},{28,12},{1,17},{... | collective-permute-start | bytes 98312 | tf_op jit(solution)/shard_map/ppermute | solution.py:25
  7.4 5.7 %collective-permute-start.5 = (bf16[128,128]{1,0:T(8,128)(2,1)S(1)}, bf16[128,128]{1,0:T(8,128)(2,1)S(1)}, u32[]{:S(2)}, u32[]{:S(2)}) collective-permute-start(bf16[128,128]{1,0:T(8,128)(2,1)S(1)} %get-tuple-element.76.refs_0_), channel_id=1, source_target_pairs={{0,24},{4,28},{8,16},{12,20},{16,8},{20,12},{24,0},{28,4},{1,25},{... | collective-permute-start | bytes 98312 | tf_op jit(solution)/shard_map/ppermute | solution.py:25
  7.4 13.6 %collective-permute-start.2 = (bf16[128,128]{1,0:T(8,128)(2,1)S(1)}, bf16[128,128]{1,0:T(8,128)(2,1)S(1)}, u32[]{:S(2)}, u32[]{:S(2)}) collective-permute-start(bf16[128,128]{1,0:T(8,128)(2,1)S(1)} %collective-permute-done.1.refs_2_), channel_id=1, source_target_pairs={{0,4},{4,0},{8,12},{12,8},{16,20},{20,16},{24,28},{28,24},{1,5},{5... | collective-permute-start | bytes 98312 | tf_op jit(solution)/shard_map/ppermute | solution.py:25
  10.2 10.8 %collective-permute-start.4 = (bf16[128,128]{1,0:T(8,128)(2,1)S(1)}, bf16[128,128]{1,0:T(8,128)(2,1)S(1)}, u32[]{:S(2)}, u32[]{:S(2)}) collective-permute-start(bf16[128,128]{1,0:T(8,128)(2,1)S(1)} %collective-permute-done.3.refs_4_), channel_id=1, source_target_pairs={{0,4},{4,0},{8,12},{12,8},{16,20},{20,16},{24,28},{28,24},{1,5},{5... | collective-permute-start | bytes 98312 | tf_op jit(solution)/shard_map/ppermute | solution.py:25
  13.1 7.9 %collective-permute-start.6 = (bf16[128,128]{1,0:T(8,128)(2,1)S(1)}, bf16[128,128]{1,0:T(8,128)(2,1)S(1)}, u32[]{:S(2)}, u32[]{:S(2)}) collective-permute-start(bf16[128,128]{1,0:T(8,128)(2,1)S(1)} %collective-permute-done.5.refs_6_), channel_id=1, source_target_pairs={{0,4},{4,0},{8,12},{12,8},{16,20},{20,16},{24,28},{28,24},{1,5},{5... | collective-permute-start | bytes 98312 | tf_op jit(solution)/shard_map/ppermute | solution.py:25
  14.6 6.4 %collective-permute-start = (bf16[128,128]{1,0:T(8,128)(2,1)S(1)}, bf16[128,128]{1,0:T(8,128)(2,1)S(1)}, u32[]{:S(2)}, u32[]{:S(2)}) collective-permute-start(bf16[128,128]{1,0:T(8,128)(2,1)S(1)} %get-tuple-element.76.refs_0_), channel_id=1, source_target_pairs={{0,4},{4,0},{8,12},{12,8},{16,20},{20,16},{24,28},{28,24},{1,5},{5... | collective-permute-start | bytes 98312 | tf_op jit(solution)/shard_map/ppermute | solution.py:25
  21.4 1.4 %collective-permute-start.8 = (bf16[128,512]{1,0:T(8,128)(2,1)S(1)}, bf16[128,512]{1,0:T(8,128)(2,1)S(1)}, u32[]{:S(2)}, u32[]{:S(2)}) collective-permute-start(bf16[128,512]{1,0:T(8,128)(2,1)S(1)} %shard_map.99), channel_id=1, source_target_pairs={{0,1},{1,0},{2,3},{3,2},{4,5},{5,4},{6,7},{7,6},{8,9},{9,8},{10,11... | collective-permute-start | bytes 393224 | tf_op jit(solution)/shard_map/ppermute | solution.py:25
  21.8 1.9 %collective-permute-start.7 = (bf16[128,512]{1,0:T(8,128)(2,1)S(1)}, bf16[128,512]{1,0:T(8,128)(2,1)S(1)}, u32[]{:S(2)}, u32[]{:S(2)}) collective-permute-start(bf16[128,512]{1,0:T(8,128)(2,1)S(1)} %shard_map.98), channel_id=1, source_target_pairs={{0,1},{1,0},{2,3},{3,2},{4,5},{5,4},{6,7},{7,6},{8,9},{9,8},{10,11... | collective-permute-start | bytes 393224 | tf_op jit(solution)/shard_map/ppermute | solution.py:25
  23.5 3.3 %collective-permute-start.12 = (bf16[128,512]{1,0:T(8,128)(2,1)S(1)}, bf16[128,512]{1,0:T(8,128)(2,1)S(1)}, u32[]{:S(2)}, u32[]{:S(2)}) collective-permute-start(bf16[128,512]{1,0:T(8,128)(2,1)S(1)} %shard_map.101), channel_id=1, source_target_pairs={{0,1},{1,0},{2,3},{3,2},{4,5},{5,4},{6,7},{7,6},{8,9},{9,8},{10,11... | collective-permute-start | bytes 393224 | tf_op jit(solution)/shard_map/ppermute | solution.py:25
  24.4 2.9 %collective-permute-start.9 = (bf16[128,512]{1,0:T(8,128)(2,1)S(1)}, bf16[128,512]{1,0:T(8,128)(2,1)S(1)}, u32[]{:S(2)}, u32[]{:S(2)}) collective-permute-start(bf16[128,512]{1,0:T(8,128)(2,1)S(1)} %shard_map.103), channel_id=1, source_target_pairs={{0,1},{1,0},{2,3},{3,2},{4,5},{5,4},{6,7},{7,6},{8,9},{9,8},{10,11... | collective-permute-start | bytes 393224 | tf_op jit(solution)/shard_map/ppermute | solution.py:25
  24.8 6.4 %collective-permute-start.17 = (bf16[128,512]{1,0:T(8,128)(2,1)S(1)}, bf16[128,512]{1,0:T(8,128)(2,1)S(1)}, u32[]{:S(2)}, u32[]{:S(2)}) collective-permute-start(bf16[128,512]{1,0:T(8,128)(2,1)S(1)} %get-tuple-element.96), channel_id=1, source_target_pairs={{0,2},{1,3},{2,0},{3,1},{4,6},{5,7},{6,4},{7,5},{8,10},{9,11},{10,... | collective-permute-start | bytes 393224 | tf_op jit(solution)/shard_map/ppermute | solution.py:25
  24.8 6.4 %copy-start = (f32[4096]{0:T(1024)S(1)}, f32[4096]{0:T(1024)}, u32[]{:S(2)}) copy-start(f32[4096]{0:T(1024)} %param.13) | copy-start | bytes 49156
  24.8 9.2 %collective-permute-start.15 = (bf16[128,512]{1,0:T(8,128)(2,1)S(1)}, bf16[128,512]{1,0:T(8,128)(2,1)S(1)}, u32[]{:S(2)}, u32[]{:S(2)}) collective-permute-start(bf16[128,512]{1,0:T(8,128)(2,1)S(1)} %get-tuple-element.94), channel_id=1, source_target_pairs={{0,2},{1,3},{2,0},{3,1},{4,6},{5,7},{6,4},{7,5},{8,10},{9,11},{10,... | collective-permute-start | bytes 393224 | tf_op jit(solution)/shard_map/ppermute | solution.py:25
  27.1 9.6 %collective-permute-start.13 = (bf16[128,512]{1,0:T(8,128)(2,1)S(1)}, bf16[128,512]{1,0:T(8,128)(2,1)S(1)}, u32[]{:S(2)}, u32[]{:S(2)}) collective-permute-start(bf16[128,512]{1,0:T(8,128)(2,1)S(1)} %get-tuple-element.92), channel_id=1, source_target_pairs={{0,2},{1,3},{2,0},{3,1},{4,6},{5,7},{6,4},{7,5},{8,10},{9,11},{10,... | collective-permute-start | bytes 393224 | tf_op jit(solution)/shard_map/ppermute | solution.py:25
  27.6 11.2 %collective-permute-start.10 = (bf16[128,512]{1,0:T(8,128)(2,1)S(1)}, bf16[128,512]{1,0:T(8,128)(2,1)S(1)}, u32[]{:S(2)}, u32[]{:S(2)}) collective-permute-start(bf16[128,512]{1,0:T(8,128)(2,1)S(1)} %get-tuple-element.88), channel_id=1, source_target_pairs={{0,2},{1,3},{2,0},{3,1},{4,6},{5,7},{6,4},{7,5},{8,10},{9,11},{10,... | collective-permute-start | bytes 393224 | tf_op jit(solution)/shard_map/ppermute | solution.py:25
  31.2 7.7 %collective-permute-start.18 = (bf16[128,512]{1,0:T(8,128)(2,1)S(1)}, bf16[128,512]{1,0:T(8,128)(2,1)S(1)}, u32[]{:S(2)}, u32[]{:S(2)}) collective-permute-start(bf16[128,512]{1,0:T(8,128)(2,1)S(1)} %shard_map.109.refs_1_), channel_id=1, source_target_pairs={{0,1},{1,0},{2,3},{3,2},{4,5},{5,4},{6,7},{7,6},{8,9},{9,8},{10,11... | collective-permute-start | bytes 393224 | tf_op jit(solution)/shard_map/ppermute | solution.py:25
  34.0 5.7 %collective-permute-start.16 = (bf16[128,512]{1,0:T(8,128)(2,1)S(1)}, bf16[128,512]{1,0:T(8,128)(2,1)S(1)}, u32[]{:S(2)}, u32[]{:S(2)}) collective-permute-start(bf16[128,512]{1,0:T(8,128)(2,1)S(1)} %shard_map.108.refs_1_), channel_id=1, source_target_pairs={{0,1},{1,0},{2,3},{3,2},{4,5},{5,4},{6,7},{7,6},{8,9},{9,8},{10,11... | collective-permute-start | bytes 393224 | tf_op jit(solution)/shard_map/ppermute | solution.py:25
  36.8 3.8 %collective-permute-start.14 = (bf16[128,512]{1,0:T(8,128)(2,1)S(1)}, bf16[128,512]{1,0:T(8,128)(2,1)S(1)}, u32[]{:S(2)}, u32[]{:S(2)}) collective-permute-start(bf16[128,512]{1,0:T(8,128)(2,1)S(1)} %shard_map.107.refs_1_), channel_id=1, source_target_pairs={{0,1},{1,0},{2,3},{3,2},{4,5},{5,4},{6,7},{7,6},{8,9},{9,8},{10,11... | collective-permute-start | bytes 393224 | tf_op jit(solution)/shard_map/ppermute | solution.py:25
  38.8 3.1 %collective-permute-start.11 = (bf16[128,512]{1,0:T(8,128)(2,1)S(1)}, bf16[128,512]{1,0:T(8,128)(2,1)S(1)}, u32[]{:S(2)}, u32[]{:S(2)}) collective-permute-start(bf16[128,512]{1,0:T(8,128)(2,1)S(1)} %shard_map.105.refs_1_), channel_id=1, source_target_pairs={{0,1},{1,0},{2,3},{3,2},{4,5},{5,4},{6,7},{7,6},{8,9},{9,8},{10,11... | collective-permute-start | bytes 393224 | tf_op jit(solution)/shard_map/ppermute | solution.py:25
  41.4 15.1 %copy-start.1 = (f32[1,128]{1,0:T(1,128)S(1)}, f32[1,128]{1,0:T(1,128)}, u32[]{:S(2)}) copy-start(f32[1,128]{1,0:T(1,128)} %refs_4_.3) | copy-start | bytes 1540
  42.4 6.4 %collective-permute-start.21 = (f32[128,256]{1,0:T(8,128)S(1)}, f32[128,256]{1,0:T(8,128)S(1)}, u32[]{:S(2)}, u32[]{:S(2)}) collective-permute-start(f32[128,256]{1,0:T(8,128)S(1)} %get-tuple-element.102), channel_id=1, source_target_pairs={{0,4},{4,0},{8,12},{12,8},{16,20},{20,16},{24,28},{28,24},{1,5},{5... | collective-permute-start | bytes 393224 | tf_op jit(solution)/shard_map/ppermute | solution.py:25
  42.8 8.4 %collective-permute-start.19 = (f32[128,256]{1,0:T(8,128)S(1)}, f32[128,256]{1,0:T(8,128)S(1)}, u32[]{:S(2)}, u32[]{:S(2)}) collective-permute-start(f32[128,256]{1,0:T(8,128)S(1)} %get-tuple-element.98), channel_id=1, source_target_pairs={{0,4},{4,0},{8,12},{12,8},{16,20},{20,16},{24,28},{28,24},{1,5},{5... | collective-permute-start | bytes 393224 | tf_op jit(solution)/shard_map/ppermute | solution.py:25
  48.9 5.9 %collective-permute-start.22 = (f32[128,128]{1,0:T(8,128)S(1)}, f32[128,128]{1,0:T(8,128)S(1)}, u32[]{:S(2)}, u32[]{:S(2)}) collective-permute-start(f32[128,128]{1,0:T(8,128)S(1)} %get-tuple-element.106), channel_id=1, source_target_pairs={{0,16},{4,20},{8,24},{12,28},{16,0},{20,4},{24,8},{28,12},{1,17},{... | collective-permute-start | bytes 196616 | tf_op jit(solution)/shard_map/ppermute | solution.py:25
  49.4 6.2 %collective-permute-start.23 = (f32[128,128]{1,0:T(8,128)S(1)}, f32[128,128]{1,0:T(8,128)S(1)}, u32[]{:S(2)}, u32[]{:S(2)}) collective-permute-start(f32[128,128]{1,0:T(8,128)S(1)} %get-tuple-element.107), channel_id=1, source_target_pairs={{0,24},{4,28},{8,16},{12,20},{16,8},{20,12},{24,0},{28,4},{1,25},{... | collective-permute-start | bytes 196616 | tf_op jit(solution)/shard_map/ppermute | solution.py:25
  51.2 5.3 %collective-permute-start.20 = (f32[128,128]{1,0:T(8,128)S(1)}, f32[128,128]{1,0:T(8,128)S(1)}, u32[]{:S(2)}, u32[]{:S(2)}) collective-permute-start(f32[128,128]{1,0:T(8,128)S(1)} %get-tuple-element.101), channel_id=1, source_target_pairs={{0,8},{4,12},{8,0},{12,4},{16,24},{20,28},{24,16},{28,20},{1,9},{5... | collective-permute-start | bytes 196616 | tf_op jit(solution)/shard_map/ppermute | solution.py:25
  67.6 5.1 %collective-permute-start.25 = (bf16[128,128]{1,0:T(8,128)(2,1)S(1)}, bf16[128,128]{1,0:T(8,128)(2,1)S(1)}, u32[]{:S(2)}, u32[]{:S(2)}) collective-permute-start(bf16[128,128]{1,0:T(8,128)(2,1)S(1)} %get-tuple-element.111.refs_0_), channel_id=1, source_target_pairs={{0,8},{4,12},{8,0},{12,4},{16,24},{20,28},{24,16},{28,20},{1,9},{5... | collective-permute-start | bytes 98312 | tf_op jit(solution)/shard_map/ppermute | solution.py:25
  68.4 5.8 %collective-permute-start.27 = (bf16[128,128]{1,0:T(8,128)(2,1)S(1)}, bf16[128,128]{1,0:T(8,128)(2,1)S(1)}, u32[]{:S(2)}, u32[]{:S(2)}) collective-permute-start(bf16[128,128]{1,0:T(8,128)(2,1)S(1)} %get-tuple-element.111.refs_0_), channel_id=1, source_target_pairs={{0,16},{4,20},{8,24},{12,28},{16,0},{20,4},{24,8},{28,12},{1,17},{... | collective-permute-start | bytes 98312 | tf_op jit(solution)/shard_map/ppermute | solution.py:25
  69.6 5.7 %collective-permute-start.29 = (bf16[128,128]{1,0:T(8,128)(2,1)S(1)}, bf16[128,128]{1,0:T(8,128)(2,1)S(1)}, u32[]{:S(2)}, u32[]{:S(2)}) collective-permute-start(bf16[128,128]{1,0:T(8,128)(2,1)S(1)} %get-tuple-element.111.refs_0_), channel_id=1, source_target_pairs={{0,24},{4,28},{8,16},{12,20},{16,8},{20,12},{24,0},{28,4},{1,25},{... | collective-permute-start | bytes 98312 | tf_op jit(solution)/shard_map/ppermute | solution.py:25
  72.1 4.3 %collective-permute-start.24 = (bf16[128,128]{1,0:T(8,128)(2,1)S(1)}, bf16[128,128]{1,0:T(8,128)(2,1)S(1)}, u32[]{:S(2)}, u32[]{:S(2)}) collective-permute-start(bf16[128,128]{1,0:T(8,128)(2,1)S(1)} %get-tuple-element.111.refs_0_), channel_id=1, source_target_pairs={{0,4},{4,0},{8,12},{12,8},{16,20},{20,16},{24,28},{28,24},{1,5},{5... | collective-permute-start | bytes 98312 | tf_op jit(solution)/shard_map/ppermute | solution.py:25
  72.8 4.2 %collective-permute-start.26 = (bf16[128,128]{1,0:T(8,128)(2,1)S(1)}, bf16[128,128]{1,0:T(8,128)(2,1)S(1)}, u32[]{:S(2)}, u32[]{:S(2)}) collective-permute-start(bf16[128,128]{1,0:T(8,128)(2,1)S(1)} %collective-permute-done.25.refs_2_), channel_id=1, source_target_pairs={{0,4},{4,0},{8,12},{12,8},{16,20},{20,16},{24,28},{28,24},{1,5},{5... | collective-permute-start | bytes 98312 | tf_op jit(solution)/shard_map/ppermute | solution.py:25
  74.1 3.9 %collective-permute-start.28 = (bf16[128,128]{1,0:T(8,128)(2,1)S(1)}, bf16[128,128]{1,0:T(8,128)(2,1)S(1)}, u32[]{:S(2)}, u32[]{:S(2)}) collective-permute-start(bf16[128,128]{1,0:T(8,128)(2,1)S(1)} %collective-permute-done.27.refs_4_), channel_id=1, source_target_pairs={{0,4},{4,0},{8,12},{12,8},{16,20},{20,16},{24,28},{28,24},{1,5},{5... | collective-permute-start | bytes 98312 | tf_op jit(solution)/shard_map/ppermute | solution.py:25
  75.3 3.9 %collective-permute-start.30 = (bf16[128,128]{1,0:T(8,128)(2,1)S(1)}, bf16[128,128]{1,0:T(8,128)(2,1)S(1)}, u32[]{:S(2)}, u32[]{:S(2)}) collective-permute-start(bf16[128,128]{1,0:T(8,128)(2,1)S(1)} %collective-permute-done.29.refs_6_), channel_id=1, source_target_pairs={{0,4},{4,0},{8,12},{12,8},{16,20},{20,16},{24,28},{28,24},{1,5},{5... | collective-permute-start | bytes 98312 | tf_op jit(solution)/shard_map/ppermute | solution.py:25
  79.6 1.4 %collective-permute-start.32 = (bf16[128,512]{1,0:T(8,128)(2,1)S(1)}, bf16[128,512]{1,0:T(8,128)(2,1)S(1)}, u32[]{:S(2)}, u32[]{:S(2)}) collective-permute-start(bf16[128,512]{1,0:T(8,128)(2,1)S(1)} %shard_map.122), channel_id=1, source_target_pairs={{0,1},{1,0},{2,3},{3,2},{4,5},{5,4},{6,7},{7,6},{8,9},{9,8},{10,11... | collective-permute-start | bytes 393224 | tf_op jit(solution)/shard_map/ppermute | solution.py:25
  80.1 1.9 %collective-permute-start.31 = (bf16[128,512]{1,0:T(8,128)(2,1)S(1)}, bf16[128,512]{1,0:T(8,128)(2,1)S(1)}, u32[]{:S(2)}, u32[]{:S(2)}) collective-permute-start(bf16[128,512]{1,0:T(8,128)(2,1)S(1)} %shard_map.121), channel_id=1, source_target_pairs={{0,1},{1,0},{2,3},{3,2},{4,5},{5,4},{6,7},{7,6},{8,9},{9,8},{10,11... | collective-permute-start | bytes 393224 | tf_op jit(solution)/shard_map/ppermute | solution.py:25
  81.7 3.3 %collective-permute-start.36 = (bf16[128,512]{1,0:T(8,128)(2,1)S(1)}, bf16[128,512]{1,0:T(8,128)(2,1)S(1)}, u32[]{:S(2)}, u32[]{:S(2)}) collective-permute-start(bf16[128,512]{1,0:T(8,128)(2,1)S(1)} %shard_map.124), channel_id=1, source_target_pairs={{0,1},{1,0},{2,3},{3,2},{4,5},{5,4},{6,7},{7,6},{8,9},{9,8},{10,11... | collective-permute-start | bytes 393224 | tf_op jit(solution)/shard_map/ppermute | solution.py:25
  82.6 3.2 %collective-permute-start.33 = (bf16[128,512]{1,0:T(8,128)(2,1)S(1)}, bf16[128,512]{1,0:T(8,128)(2,1)S(1)}, u32[]{:S(2)}, u32[]{:S(2)}) collective-permute-start(bf16[128,512]{1,0:T(8,128)(2,1)S(1)} %shard_map.126), channel_id=1, source_target_pairs={{0,1},{1,0},{2,3},{3,2},{4,5},{5,4},{6,7},{7,6},{8,9},{9,8},{10,11... | collective-permute-start | bytes 393224 | tf_op jit(solution)/shard_map/ppermute | solution.py:25
  83.0 6.4 %collective-permute-start.41 = (bf16[128,512]{1,0:T(8,128)(2,1)S(1)}, bf16[128,512]{1,0:T(8,128)(2,1)S(1)}, u32[]{:S(2)}, u32[]{:S(2)}) collective-permute-start(bf16[128,512]{1,0:T(8,128)(2,1)S(1)} %get-tuple-element.128), channel_id=1, source_target_pairs={{0,2},{1,3},{2,0},{3,1},{4,6},{5,7},{6,4},{7,5},{8,10},{9,11},{10,... | collective-permute-start | bytes 393224 | tf_op jit(solution)/shard_map/ppermute | solution.py:25
  83.4 8.8 %collective-permute-start.39 = (bf16[128,512]{1,0:T(8,128)(2,1)S(1)}, bf16[128,512]{1,0:T(8,128)(2,1)S(1)}, u32[]{:S(2)}, u32[]{:S(2)}) collective-permute-start(bf16[128,512]{1,0:T(8,128)(2,1)S(1)} %get-tuple-element.126), channel_id=1, source_target_pairs={{0,2},{1,3},{2,0},{3,1},{4,6},{5,7},{6,4},{7,5},{8,10},{9,11},{10,... | collective-permute-start | bytes 393224 | tf_op jit(solution)/shard_map/ppermute | solution.py:25
  85.4 9.6 %collective-permute-start.37 = (bf16[128,512]{1,0:T(8,128)(2,1)S(1)}, bf16[128,512]{1,0:T(8,128)(2,1)S(1)}, u32[]{:S(2)}, u32[]{:S(2)}) collective-permute-start(bf16[128,512]{1,0:T(8,128)(2,1)S(1)} %get-tuple-element.124), channel_id=1, source_target_pairs={{0,2},{1,3},{2,0},{3,1},{4,6},{5,7},{6,4},{7,5},{8,10},{9,11},{10,... | collective-permute-start | bytes 393224 | tf_op jit(solution)/shard_map/ppermute | solution.py:25
  86.2 10.8 %collective-permute-start.34 = (bf16[128,512]{1,0:T(8,128)(2,1)S(1)}, bf16[128,512]{1,0:T(8,128)(2,1)S(1)}, u32[]{:S(2)}, u32[]{:S(2)}) collective-permute-start(bf16[128,512]{1,0:T(8,128)(2,1)S(1)} %get-tuple-element.120), channel_id=1, source_target_pairs={{0,2},{1,3},{2,0},{3,1},{4,6},{5,7},{6,4},{7,5},{8,10},{9,11},{10,... | collective-permute-start | bytes 393224 | tf_op jit(solution)/shard_map/ppermute | solution.py:25
  89.4 7.7 %collective-permute-start.42 = (bf16[128,512]{1,0:T(8,128)(2,1)S(1)}, bf16[128,512]{1,0:T(8,128)(2,1)S(1)}, u32[]{:S(2)}, u32[]{:S(2)}) collective-permute-start(bf16[128,512]{1,0:T(8,128)(2,1)S(1)} %shard_map.132.refs_1_), channel_id=1, source_target_pairs={{0,1},{1,0},{2,3},{3,2},{4,5},{5,4},{6,7},{7,6},{8,9},{9,8},{10,11... | collective-permute-start | bytes 393224 | tf_op jit(solution)/shard_map/ppermute | solution.py:25
  92.2 5.7 %collective-permute-start.40 = (bf16[128,512]{1,0:T(8,128)(2,1)S(1)}, bf16[128,512]{1,0:T(8,128)(2,1)S(1)}, u32[]{:S(2)}, u32[]{:S(2)}) collective-permute-start(bf16[128,512]{1,0:T(8,128)(2,1)S(1)} %shard_map.131.refs_1_), channel_id=1, source_target_pairs={{0,1},{1,0},{2,3},{3,2},{4,5},{5,4},{6,7},{7,6},{8,9},{9,8},{10,11... | collective-permute-start | bytes 393224 | tf_op jit(solution)/shard_map/ppermute | solution.py:25
  95.1 3.8 %collective-permute-start.38 = (bf16[128,512]{1,0:T(8,128)(2,1)S(1)}, bf16[128,512]{1,0:T(8,128)(2,1)S(1)}, u32[]{:S(2)}, u32[]{:S(2)}) collective-permute-start(bf16[128,512]{1,0:T(8,128)(2,1)S(1)} %shard_map.130.refs_1_), channel_id=1, source_target_pairs={{0,1},{1,0},{2,3},{3,2},{4,5},{5,4},{6,7},{7,6},{8,9},{9,8},{10,11... | collective-permute-start | bytes 393224 | tf_op jit(solution)/shard_map/ppermute | solution.py:25
  97.0 3.1 %collective-permute-start.35 = (bf16[128,512]{1,0:T(8,128)(2,1)S(1)}, bf16[128,512]{1,0:T(8,128)(2,1)S(1)}, u32[]{:S(2)}, u32[]{:S(2)}) collective-permute-start(bf16[128,512]{1,0:T(8,128)(2,1)S(1)} %shard_map.128.refs_1_), channel_id=1, source_target_pairs={{0,1},{1,0},{2,3},{3,2},{4,5},{5,4},{6,7},{7,6},{8,9},{9,8},{10,11... | collective-permute-start | bytes 393224 | tf_op jit(solution)/shard_map/ppermute | solution.py:25
  100.7 6.4 %collective-permute-start.45 = (f32[128,256]{1,0:T(8,128)S(1)}, f32[128,256]{1,0:T(8,128)S(1)}, u32[]{:S(2)}, u32[]{:S(2)}) collective-permute-start(f32[128,256]{1,0:T(8,128)S(1)} %get-tuple-element.134), channel_id=1, source_target_pairs={{0,4},{4,0},{8,12},{12,8},{16,20},{20,16},{24,28},{28,24},{1,5},{5... | collective-permute-start | bytes 393224 | tf_op jit(solution)/shard_map/ppermute | solution.py:25
  101.6 8.2 %collective-permute-start.43 = (f32[128,256]{1,0:T(8,128)S(1)}, f32[128,256]{1,0:T(8,128)S(1)}, u32[]{:S(2)}, u32[]{:S(2)}) collective-permute-start(f32[128,256]{1,0:T(8,128)S(1)} %get-tuple-element.130), channel_id=1, source_target_pairs={{0,4},{4,0},{8,12},{12,8},{16,20},{20,16},{24,28},{28,24},{1,5},{5... | collective-permute-start | bytes 393224 | tf_op jit(solution)/shard_map/ppermute | solution.py:25
  107.1 7.2 %collective-permute-start.46 = (f32[128,128]{1,0:T(8,128)S(1)}, f32[128,128]{1,0:T(8,128)S(1)}, u32[]{:S(2)}, u32[]{:S(2)}) collective-permute-start(f32[128,128]{1,0:T(8,128)S(1)} %get-tuple-element.138), channel_id=1, source_target_pairs={{0,16},{4,20},{8,24},{12,28},{16,0},{20,4},{24,8},{28,12},{1,17},{... | collective-permute-start | bytes 196616 | tf_op jit(solution)/shard_map/ppermute | solution.py:25
  107.2 7.1 %collective-permute-start.47 = (f32[128,128]{1,0:T(8,128)S(1)}, f32[128,128]{1,0:T(8,128)S(1)}, u32[]{:S(2)}, u32[]{:S(2)}) collective-permute-start(f32[128,128]{1,0:T(8,128)S(1)} %get-tuple-element.139), channel_id=1, source_target_pairs={{0,24},{4,28},{8,16},{12,20},{16,8},{20,12},{24,0},{28,4},{1,25},{... | collective-permute-start | bytes 196616 | tf_op jit(solution)/shard_map/ppermute | solution.py:25
  109.8 5.0 %collective-permute-start.44 = (f32[128,128]{1,0:T(8,128)S(1)}, f32[128,128]{1,0:T(8,128)S(1)}, u32[]{:S(2)}, u32[]{:S(2)}) collective-permute-start(f32[128,128]{1,0:T(8,128)S(1)} %get-tuple-element.133), channel_id=1, source_target_pairs={{0,8},{4,12},{8,0},{12,4},{16,24},{20,28},{24,16},{28,20},{1,9},{5... | collective-permute-start | bytes 196616 | tf_op jit(solution)/shard_map/ppermute | solution.py:25

commit v2 on v1

--- a/solution.py
+++ b/solution.py
@@ -145,15 +145,16 @@
                 q, b = split(col, share_blocks)
                 lane = pl.multiple_of(b * bs, bs)
 
-                @pl.when(live_ref[0, k] == 1)
+                live = live_ref[0, k] == 1
+                seen = seen_ref[cell]
+
+                @pl.when(live & (seen == -1))
                 def _():
-                    seen = seen_ref[cell]
-
-                    @pl.when(seen == -1)
-                    def _():
-                        seen_ref[cell] = -2
-                        out_ref[q, pl.ds(at, bs), pl.ds(lane, bs)] = held_ref[k]
-
+                    seen_ref[cell] = -2
+                    out_ref[q, pl.ds(at, bs), pl.ds(lane, bs)] = held_ref[k]
+
+                @pl.when(live & (seen != -1))
+                def _():
                     @pl.when(seen == -2)
                     def _():
                         seen_ref[cell] = k
@@ -171,7 +172,7 @@
 
             for f in range(fetches):
                 copies[f].wait()
-                lax.fori_loop(f * batch, (f + 1) * batch, add, 0, unroll=4)
+                lax.fori_loop(f * batch, (f + 1) * batch, add, 0, unroll=8)
 
         def clear_body(out_ref):
             def clear(i, carry):

time: 127 us -> 127 us (level)
  transfers between devices with their start and end apart: 48 -> 48, of which waited for: 25 -> 25; matrix products, arithmetic and copies ran while one was open for 0% -> 0% of each run, Pallas kernels for 14% -> 13%
where the time goes in v2:
time: 127 us
  waiting for transfers between devices  41.5 us (33%)
  starting transfers between devices  41.1 us (32%)
  blocking collectives  22.1 us (17%)
  Pallas kernels  20.7 us (16%)
    ppermute x48, waiting for transfers between devices, xor_permute(): return lax.ppermute(array, axis, [(i, i ^ bit) for i in range(count)])  41.5 us
    ppermute x48, starting transfers between devices, xor_permute(): return lax.ppermute(array, axis, [(i, i ^ bit) for i in range(count)])  41.1 us
    all_to_all x2, blocking collectives, everywhere(): return lax.all_to_all(tile, ('src', 'tm'), 0, 0, tiled=True)  22.1 us
    pallas_call x8, Pallas kernels, forward_part(): kernel(body, sds((ds, wrows)), 1 + len(scaled) + len(more), placed=True,...  5.92 us
    pallas_call x16, Pallas kernels, adjoint_part(): kernel(body, (shape, sds((ds, width))) if more else shape, 2 + len(more),...  5.13 us
    pallas_call x1, Pallas kernels, build(): kernel(body, pltpu.VMEM((windows, wrows, share), BF), 5, in_specs=[hbm] *...  4.68 us
  transfers between devices with their start and end apart: 48, of which 25 were waited for; matrix products, arithmetic and copies ran while one was open for 0% of the time, Pallas kernels for 13%

profile of v2, /device:TPU:0, one launch (start us, length us, event | category | flops | bytes accessed | tf_op | source)
XLA Modules:
  0.0 126.5 jit_solution(10664440850253346836)
XLA Ops:
  0.6 1.0 shard_map.96
  1.7 3.1 %collective-permute-start.1 = (bf16[128,128]{1,0:T(8,128)(2,1)S(1)}, bf16[128,128]{1,0:T(8,128)(2,1)S(1)}, u32[]{:S(2)}, u32[]{:S(2)}) collective-permute-start(bf16[128,128]{1,0:T(8,128)(2,1)S(1)} %get-tuple-element.76.refs_0_), channel_id=1, source_target_pairs={{0,8},{4,12},{8,0},{12,4},{16,24},{20,28},{24,16},{28,20},{1,9},{5... | collective-permute-start | bytes 98312 | tf_op jit(solution)/shard_map/ppermute | solution.py:25
  4.8 2.6 %collective-permute-start.3 = (bf16[128,128]{1,0:T(8,128)(2,1)S(1)}, bf16[128,128]{1,0:T(8,128)(2,1)S(1)}, u32[]{:S(2)}, u32[]{:S(2)}) collective-permute-start(bf16[128,128]{1,0:T(8,128)(2,1)S(1)} %get-tuple-element.76.refs_0_), channel_id=1, source_target_pairs={{0,16},{4,20},{8,24},{12,28},{16,0},{20,4},{24,8},{28,12},{1,17},{... | collective-permute-start | bytes 98312 | tf_op jit(solution)/shard_map/ppermute | solution.py:25
  7.4 1.7 %collective-permute-start.2 = (bf16[128,128]{1,0:T(8,128)(2,1)S(1)}, bf16[128,128]{1,0:T(8,128)(2,1)S(1)}, u32[]{:S(2)}, u32[]{:S(2)}) collective-permute-start(bf16[128,128]{1,0:T(8,128)(2,1)S(1)} %collective-permute-done.1.refs_2_), channel_id=1, source_target_pairs={{0,4},{4,0},{8,12},{12,8},{16,20},{20,16},{24,28},{28,24},{1,5},{5... | collective-permute-start | bytes 98312 | tf_op jit(solution)/shard_map/ppermute | solution.py:25
  9.1 1.1 collective-permute-done.3.refs_4_
  10.2 1.5 %collective-permute-start.4 = (bf16[128,128]{1,0:T(8,128)(2,1)S(1)}, bf16[128,128]{1,0:T(8,128)(2,1)S(1)}, u32[]{:S(2)}, u32[]{:S(2)}) collective-permute-start(bf16[128,128]{1,0:T(8,128)(2,1)S(1)} %collective-permute-done.3.refs_4_), channel_id=1, source_target_pairs={{0,4},{4,0},{8,12},{12,8},{16,20},{20,16},{24,28},{28,24},{1,5},{5... | collective-permute-start | bytes 98312 | tf_op jit(solution)/shard_map/ppermute | solution.py:25
  11.7 1.4 %collective-permute-done.5.refs_6_ = bf16[128,128]{1,0:T(8,128)(2,1)S(1)} collective-permute-done((bf16[128,128]{1,0:T(8,128)(2,1)S(1)}, bf16[128,128]{1,0:T(8,128)(2,1)S(1)}, u32[]{:S(2)}, u32[]{:S(2)}) %collective-permute-start.5) | collective-permute-done | bytes 32800 | tf_op jit(solution)/shard_map/ppermute | solution.py:25
  13.1 1.5 %collective-permute-start.6 = (bf16[128,128]{1,0:T(8,128)(2,1)S(1)}, bf16[128,128]{1,0:T(8,128)(2,1)S(1)}, u32[]{:S(2)}, u32[]{:S(2)}) collective-permute-start(bf16[128,128]{1,0:T(8,128)(2,1)S(1)} %collective-permute-done.5.refs_6_), channel_id=1, source_target_pairs={{0,4},{4,0},{8,12},{12,8},{16,20},{20,16},{24,28},{28,24},{1,5},{5... | collective-permute-start | bytes 98312 | tf_op jit(solution)/shard_map/ppermute | solution.py:25
  15.1 0.6 shard_map.94._
  15.7 4.7 %shard_map.95.refs_1_.refs_0_ = bf16[4,1024,1024]{2,1,0:T(8,128)(2,1)S(1)} custom-call(s32[1,128]{1,0:T(1,128)} %rows_hbm.1, s32[1,128]{1,0:T(1,128)} %cols_hbm.1, s32[1,128]{1,0:T(1,128)} %live_hbm.1, bf16[128,128,128]{2,1,0:T(8,128)(2,1)} %bitcast.22, bf16[4,1024,1024]{2,1,0:T(8,128)(2,1)S(1)} %shard_map.94._), custom_call_target="tpu_custom_call", output_to_operand_aliasing={{}: (4, {})} | custom-call | bytes 25165824 | tf_op jit(solution)/shard_map/pallas_call | solution.py:191
  21.2 0.6 collective-permute-start.7
  24.2 0.8 collective-permute-start.17
  25.0 1.2 collective-permute-start.15
  26.5 0.8 collective-permute-start.13
  27.7 1.3 %collective-permute-start.10 = (bf16[128,512]{1,0:T(8,128)(2,1)S(1)}, bf16[128,512]{1,0:T(8,128)(2,1)S(1)}, u32[]{:S(2)}, u32[]{:S(2)}) collective-permute-start(bf16[128,512]{1,0:T(8,128)(2,1)S(1)} %get-tuple-element.88), channel_id=1, source_target_pairs={{0,2},{1,3},{2,0},{3,1},{4,6},{5,7},{6,4},{7,5},{8,10},{9,11},{10,... | collective-permute-start | bytes 393224 | tf_op jit(solution)/shard_map/ppermute | solution.py:25
  29.0 1.5 %collective-permute-done.17.refs_1_.refs_4_ = bf16[128,512]{1,0:T(8,128)(2,1)S(1)} collective-permute-done((bf16[128,512]{1,0:T(8,128)(2,1)S(1)}, bf16[128,512]{1,0:T(8,128)(2,1)S(1)}, u32[]{:S(2)}, u32[]{:S(2)}) %collective-permute-start.17) | collective-permute-done | bytes 131104 | tf_op jit(solution)/shard_map/ppermute | solution.py:25
  30.7 2.7 %collective-permute-done.15.refs_1_.refs_5_ = bf16[128,512]{1,0:T(8,128)(2,1)S(1)} collective-permute-done((bf16[128,512]{1,0:T(8,128)(2,1)S(1)}, bf16[128,512]{1,0:T(8,128)(2,1)S(1)}, u32[]{:S(2)}, u32[]{:S(2)}) %collective-permute-start.15) | collective-permute-done | bytes 131104 | tf_op jit(solution)/shard_map/ppermute | solution.py:25
  33.5 2.7 %collective-permute-done.13.refs_1_.refs_6_ = bf16[128,512]{1,0:T(8,128)(2,1)S(1)} collective-permute-done((bf16[128,512]{1,0:T(8,128)(2,1)S(1)}, bf16[128,512]{1,0:T(8,128)(2,1)S(1)}, u32[]{:S(2)}, u32[]{:S(2)}) %collective-permute-start.13) | collective-permute-done | bytes 131104 | tf_op jit(solution)/shard_map/ppermute | solution.py:25
  36.3 1.9 %collective-permute-done.10.refs_1_.refs_7_ = bf16[128,512]{1,0:T(8,128)(2,1)S(1)} collective-permute-done((bf16[128,512]{1,0:T(8,128)(2,1)S(1)}, bf16[128,512]{1,0:T(8,128)(2,1)S(1)}, u32[]{:S(2)}, u32[]{:S(2)}) %collective-permute-start.10) | collective-permute-done | bytes 131104 | tf_op jit(solution)/shard_map/ppermute | solution.py:25
  38.3 0.8 shard_map.110.refs_3_
  39.1 0.8 shard_map.111.refs_3_
  40.0 0.8 shard_map.112.refs_2_
  41.3 0.5 shard_map.114
  41.8 0.9 collective-permute-start.21
  42.8 1.1 collective-permute-start.19
  44.2 4.1 %collective-permute-done.21.refs_0_ = f32[128,256]{1,0:T(8,128)S(1)} collective-permute-done((f32[128,256]{1,0:T(8,128)S(1)}, f32[128,256]{1,0:T(8,128)S(1)}, u32[]{:S(2)}, u32[]{:S(2)}) %collective-permute-start.21) | collective-permute-done | bytes 131104 | tf_op jit(solution)/shard_map/ppermute | solution.py:25
  48.3 0.6 collective-permute-start.22
  48.9 1.0 collective-permute-start.23
  49.9 0.8 collective-permute-done.19.refs_0_
  50.6 1.3 %collective-permute-start.20 = (f32[128,128]{1,0:T(8,128)S(1)}, f32[128,128]{1,0:T(8,128)S(1)}, u32[]{:S(2)}, u32[]{:S(2)}) collective-permute-start(f32[128,128]{1,0:T(8,128)S(1)} %get-tuple-element.101), channel_id=1, source_target_pairs={{0,8},{4,12},{8,0},{12,4},{16,24},{20,28},{24,16},{28,20},{1,9},{5... | collective-permute-start | bytes 196616 | tf_op jit(solution)/shard_map/ppermute | solution.py:25
  52.0 2.3 %collective-permute-done.22.refs_2_ = f32[128,128]{1,0:T(8,128)S(1)} collective-permute-done((f32[128,128]{1,0:T(8,128)S(1)}, f32[128,128]{1,0:T(8,128)S(1)}, u32[]{:S(2)}, u32[]{:S(2)}) %collective-permute-start.22) | collective-permute-done | bytes 65568 | tf_op jit(solution)/shard_map/ppermute | solution.py:25
  54.3 0.7 collective-permute-done.23.refs_3_
  55.0 0.9 collective-permute-done.20.refs_1_
  56.1 11.0 %all_to_all.22 = f32[32,8,128]{2,1,0:T(8,128)S(1)} all-to-all(f32[32,8,128]{2,1,0:T(8,128)S(1)} %bitcast.20), channel_id=1, replica_groups=mesh['src'=8,'tm'=4] {'src','tm'}, dimensions={0} | all-to-all | bytes 262144 | tf_op jit(solution)/shard_map/all_to_all | solution.py:466
  67.2 0.7 collective-permute-start.25
  68.0 1.2 collective-permute-start.27
  69.2 2.5 %collective-permute-start.29 = (bf16[128,128]{1,0:T(8,128)(2,1)S(1)}, bf16[128,128]{1,0:T(8,128)(2,1)S(1)}, u32[]{:S(2)}, u32[]{:S(2)}) collective-permute-start(bf16[128,128]{1,0:T(8,128)(2,1)S(1)} %get-tuple-element.111.refs_0_), channel_id=1, source_target_pairs={{0,24},{4,28},{8,16},{12,20},{16,8},{20,12},{24,0},{28,4},{1,25},{... | collective-permute-start | bytes 98312 | tf_op jit(solution)/shard_map/ppermute | solution.py:25
  71.7 0.7 collective-permute-start.24
  72.4 1.4 %collective-permute-start.26 = (bf16[128,128]{1,0:T(8,128)(2,1)S(1)}, bf16[128,128]{1,0:T(8,128)(2,1)S(1)}, u32[]{:S(2)}, u32[]{:S(2)}) collective-permute-start(bf16[128,128]{1,0:T(8,128)(2,1)S(1)} %collective-permute-done.25.refs_2_), channel_id=1, source_target_pairs={{0,4},{4,0},{8,12},{12,8},{16,20},{20,16},{24,28},{28,24},{1,5},{5... | collective-permute-start | bytes 98312 | tf_op jit(solution)/shard_map/ppermute | solution.py:25
  73.7 0.7 collective-permute-start.28
  74.4 0.5 collective-permute-done.29.refs_6_
  74.9 0.8 collective-permute-start.30
  76.0 0.6 collective-permute-done.26.refs_3_
  76.5 1.1 collective-permute-done.28.refs_5_
  77.6 1.2 collective-permute-done.30.refs_7_
  79.6 0.6 collective-permute-start.31
  83.0 1.6 %collective-permute-start.39 = (bf16[128,512]{1,0:T(8,128)(2,1)S(1)}, bf16[128,512]{1,0:T(8,128)(2,1)S(1)}, u32[]{:S(2)}, u32[]{:S(2)}) collective-permute-start(bf16[128,512]{1,0:T(8,128)(2,1)S(1)} %get-tuple-element.126), channel_id=1, source_target_pairs={{0,2},{1,3},{2,0},{3,1},{4,6},{5,7},{6,4},{7,5},{8,10},{9,11},{10,... | collective-permute-start | bytes 393224 | tf_op jit(solution)/shard_map/ppermute | solution.py:25
  85.7 1.7 %collective-permute-start.34 = (bf16[128,512]{1,0:T(8,128)(2,1)S(1)}, bf16[128,512]{1,0:T(8,128)(2,1)S(1)}, u32[]{:S(2)}, u32[]{:S(2)}) collective-permute-start(bf16[128,512]{1,0:T(8,128)(2,1)S(1)} %get-tuple-element.120), channel_id=1, source_target_pairs={{0,2},{1,3},{2,0},{3,1},{4,6},{5,7},{6,4},{7,5},{8,10},{9,11},{10,... | collective-permute-start | bytes 393224 | tf_op jit(solution)/shard_map/ppermute | solution.py:25
  87.4 1.5 %collective-permute-done.41.refs_1_.refs_4_ = bf16[128,512]{1,0:T(8,128)(2,1)S(1)} collective-permute-done((bf16[128,512]{1,0:T(8,128)(2,1)S(1)}, bf16[128,512]{1,0:T(8,128)(2,1)S(1)}, u32[]{:S(2)}, u32[]{:S(2)}) %collective-permute-start.41) | collective-permute-done | bytes 131104 | tf_op jit(solution)/shard_map/ppermute | solution.py:25
  89.1 2.7 %collective-permute-done.39.refs_1_.refs_5_ = bf16[128,512]{1,0:T(8,128)(2,1)S(1)} collective-permute-done((bf16[128,512]{1,0:T(8,128)(2,1)S(1)}, bf16[128,512]{1,0:T(8,128)(2,1)S(1)}, u32[]{:S(2)}, u32[]{:S(2)}) %collective-permute-start.39) | collective-permute-done | bytes 131104 | tf_op jit(solution)/shard_map/ppermute | solution.py:25
  91.9 2.7 %collective-permute-done.37.refs_1_.refs_6_ = bf16[128,512]{1,0:T(8,128)(2,1)S(1)} collective-permute-done((bf16[128,512]{1,0:T(8,128)(2,1)S(1)}, bf16[128,512]{1,0:T(8,128)(2,1)S(1)}, u32[]{:S(2)}, u32[]{:S(2)}) %collective-permute-start.37) | collective-permute-done | bytes 131104 | tf_op jit(solution)/shard_map/ppermute | solution.py:25
  94.7 1.9 %collective-permute-done.34.refs_1_.refs_7_ = bf16[128,512]{1,0:T(8,128)(2,1)S(1)} collective-permute-done((bf16[128,512]{1,0:T(8,128)(2,1)S(1)}, bf16[128,512]{1,0:T(8,128)(2,1)S(1)}, u32[]{:S(2)}, u32[]{:S(2)}) %collective-permute-start.34) | collective-permute-done | bytes 131104 | tf_op jit(solution)/shard_map/ppermute | solution.py:25
  96.7 0.8 shard_map.133.refs_3_
  97.5 0.8 shard_map.134.refs_3_
  98.4 0.8 shard_map.135.refs_2_
  100.2 0.9 collective-permute-start.45
  101.2 1.2 collective-permute-start.43
  102.6 4.1 %collective-permute-done.45.refs_0_ = f32[128,256]{1,0:T(8,128)S(1)} collective-permute-done((f32[128,256]{1,0:T(8,128)S(1)}, f32[128,256]{1,0:T(8,128)S(1)}, u32[]{:S(2)}, u32[]{:S(2)}) %collective-permute-start.45) | collective-permute-done | bytes 131104 | tf_op jit(solution)/shard_map/ppermute | solution.py:25
  106.8 2.6 %collective-permute-start.47 = (f32[128,128]{1,0:T(8,128)S(1)}, f32[128,128]{1,0:T(8,128)S(1)}, u32[]{:S(2)}, u32[]{:S(2)}) collective-permute-start(f32[128,128]{1,0:T(8,128)S(1)} %get-tuple-element.139), channel_id=1, source_target_pairs={{0,24},{4,28},{8,16},{12,20},{16,8},{20,12},{24,0},{28,4},{1,25},{... | collective-permute-start | bytes 196616 | tf_op jit(solution)/shard_map/ppermute | solution.py:25
  109.4 1.0 collective-permute-start.44
  110.4 3.5 %collective-permute-done.46.refs_2_ = f32[128,128]{1,0:T(8,128)S(1)} collective-permute-done((f32[128,128]{1,0:T(8,128)S(1)}, f32[128,128]{1,0:T(8,128)S(1)}, u32[]{:S(2)}, u32[]{:S(2)}) %collective-permute-start.46) | collective-permute-done | bytes 65568 | tf_op jit(solution)/shard_map/ppermute | solution.py:25
  113.9 0.5 collective-permute-done.44.refs_1_
  114.6 11.1 %all_to_all.23 = f32[32,8,128]{2,1,0:T(8,128)S(1)} all-to-all(f32[32,8,128]{2,1,0:T(8,128)S(1)} %bitcast.21), channel_id=1, replica_groups=mesh['src'=8,'tm'=4] {'src','tm'}, dimensions={0} | all-to-all | bytes 262144 | tf_op jit(solution)/shard_map/all_to_all | solution.py:466
  125.6 0.9 shard_map.142
  (87 shorter events, 12.6 us)
Async XLA Ops:
  1.7 5.7 %collective-permute-start.1 = (bf16[128,128]{1,0:T(8,128)(2,1)S(1)}, bf16[128,128]{1,0:T(8,128)(2,1)S(1)}, u32[]{:S(2)}, u32[]{:S(2)}) collective-permute-start(bf16[128,128]{1,0:T(8,128)(2,1)S(1)} %get-tuple-element.76.refs_0_), channel_id=1, source_target_pairs={{0,8},{4,12},{8,0},{12,4},{16,24},{20,28},{24,16},{28,20},{1,9},{5... | collective-permute-start | bytes 98312 | tf_op jit(solution)/shard_map/ppermute | solution.py:25
  4.8 5.4 %collective-permute-start.3 = (bf16[128,128]{1,0:T(8,128)(2,1)S(1)}, bf16[128,128]{1,0:T(8,128)(2,1)S(1)}, u32[]{:S(2)}, u32[]{:S(2)}) collective-permute-start(bf16[128,128]{1,0:T(8,128)(2,1)S(1)} %get-tuple-element.76.refs_0_), channel_id=1, source_target_pairs={{0,16},{4,20},{8,24},{12,28},{16,0},{20,4},{24,8},{28,12},{1,17},{... | collective-permute-start | bytes 98312 | tf_op jit(solution)/shard_map/ppermute | solution.py:25
  7.4 5.7 %collective-permute-start.5 = (bf16[128,128]{1,0:T(8,128)(2,1)S(1)}, bf16[128,128]{1,0:T(8,128)(2,1)S(1)}, u32[]{:S(2)}, u32[]{:S(2)}) collective-permute-start(bf16[128,128]{1,0:T(8,128)(2,1)S(1)} %get-tuple-element.76.refs_0_), channel_id=1, source_target_pairs={{0,24},{4,28},{8,16},{12,20},{16,8},{20,12},{24,0},{28,4},{1,25},{... | collective-permute-start | bytes 98312 | tf_op jit(solution)/shard_map/ppermute | solution.py:25
  7.4 13.0 %collective-permute-start.2 = (bf16[128,128]{1,0:T(8,128)(2,1)S(1)}, bf16[128,128]{1,0:T(8,128)(2,1)S(1)}, u32[]{:S(2)}, u32[]{:S(2)}) collective-permute-start(bf16[128,128]{1,0:T(8,128)(2,1)S(1)} %collective-permute-done.1.refs_2_), channel_id=1, source_target_pairs={{0,4},{4,0},{8,12},{12,8},{16,20},{20,16},{24,28},{28,24},{1,5},{5... | collective-permute-start | bytes 98312 | tf_op jit(solution)/shard_map/ppermute | solution.py:25
  10.2 10.2 %collective-permute-start.4 = (bf16[128,128]{1,0:T(8,128)(2,1)S(1)}, bf16[128,128]{1,0:T(8,128)(2,1)S(1)}, u32[]{:S(2)}, u32[]{:S(2)}) collective-permute-start(bf16[128,128]{1,0:T(8,128)(2,1)S(1)} %collective-permute-done.3.refs_4_), channel_id=1, source_target_pairs={{0,4},{4,0},{8,12},{12,8},{16,20},{20,16},{24,28},{28,24},{1,5},{5... | collective-permute-start | bytes 98312 | tf_op jit(solution)/shard_map/ppermute | solution.py:25
  13.1 7.3 %collective-permute-start.6 = (bf16[128,128]{1,0:T(8,128)(2,1)S(1)}, bf16[128,128]{1,0:T(8,128)(2,1)S(1)}, u32[]{:S(2)}, u32[]{:S(2)}) collective-permute-start(bf16[128,128]{1,0:T(8,128)(2,1)S(1)} %collective-permute-done.5.refs_6_), channel_id=1, source_target_pairs={{0,4},{4,0},{8,12},{12,8},{16,20},{20,16},{24,28},{28,24},{1,5},{5... | collective-permute-start | bytes 98312 | tf_op jit(solution)/shard_map/ppermute | solution.py:25
  14.6 5.8 %collective-permute-start = (bf16[128,128]{1,0:T(8,128)(2,1)S(1)}, bf16[128,128]{1,0:T(8,128)(2,1)S(1)}, u32[]{:S(2)}, u32[]{:S(2)}) collective-permute-start(bf16[128,128]{1,0:T(8,128)(2,1)S(1)} %get-tuple-element.76.refs_0_), channel_id=1, source_target_pairs={{0,4},{4,0},{8,12},{12,8},{16,20},{20,16},{24,28},{28,24},{1,5},{5... | collective-permute-start | bytes 98312 | tf_op jit(solution)/shard_map/ppermute | solution.py:25
  20.8 1.4 %collective-permute-start.8 = (bf16[128,512]{1,0:T(8,128)(2,1)S(1)}, bf16[128,512]{1,0:T(8,128)(2,1)S(1)}, u32[]{:S(2)}, u32[]{:S(2)}) collective-permute-start(bf16[128,512]{1,0:T(8,128)(2,1)S(1)} %shard_map.99), channel_id=1, source_target_pairs={{0,1},{1,0},{2,3},{3,2},{4,5},{5,4},{6,7},{7,6},{8,9},{9,8},{10,11... | collective-permute-start | bytes 393224 | tf_op jit(solution)/shard_map/ppermute | solution.py:25
  21.2 1.9 %collective-permute-start.7 = (bf16[128,512]{1,0:T(8,128)(2,1)S(1)}, bf16[128,512]{1,0:T(8,128)(2,1)S(1)}, u32[]{:S(2)}, u32[]{:S(2)}) collective-permute-start(bf16[128,512]{1,0:T(8,128)(2,1)S(1)} %shard_map.98), channel_id=1, source_target_pairs={{0,1},{1,0},{2,3},{3,2},{4,5},{5,4},{6,7},{7,6},{8,9},{9,8},{10,11... | collective-permute-start | bytes 393224 | tf_op jit(solution)/shard_map/ppermute | solution.py:25
  22.9 3.3 %collective-permute-start.12 = (bf16[128,512]{1,0:T(8,128)(2,1)S(1)}, bf16[128,512]{1,0:T(8,128)(2,1)S(1)}, u32[]{:S(2)}, u32[]{:S(2)}) collective-permute-start(bf16[128,512]{1,0:T(8,128)(2,1)S(1)} %shard_map.101), channel_id=1, source_target_pairs={{0,1},{1,0},{2,3},{3,2},{4,5},{5,4},{6,7},{7,6},{8,9},{9,8},{10,11... | collective-permute-start | bytes 393224 | tf_op jit(solution)/shard_map/ppermute | solution.py:25
  23.8 3.6 %collective-permute-start.9 = (bf16[128,512]{1,0:T(8,128)(2,1)S(1)}, bf16[128,512]{1,0:T(8,128)(2,1)S(1)}, u32[]{:S(2)}, u32[]{:S(2)}) collective-permute-start(bf16[128,512]{1,0:T(8,128)(2,1)S(1)} %shard_map.103), channel_id=1, source_target_pairs={{0,1},{1,0},{2,3},{3,2},{4,5},{5,4},{6,7},{7,6},{8,9},{9,8},{10,11... | collective-permute-start | bytes 393224 | tf_op jit(solution)/shard_map/ppermute | solution.py:25
  24.2 6.4 %collective-permute-start.17 = (bf16[128,512]{1,0:T(8,128)(2,1)S(1)}, bf16[128,512]{1,0:T(8,128)(2,1)S(1)}, u32[]{:S(2)}, u32[]{:S(2)}) collective-permute-start(bf16[128,512]{1,0:T(8,128)(2,1)S(1)} %get-tuple-element.96), channel_id=1, source_target_pairs={{0,2},{1,3},{2,0},{3,1},{4,6},{5,7},{6,4},{7,5},{8,10},{9,11},{10,... | collective-permute-start | bytes 393224 | tf_op jit(solution)/shard_map/ppermute | solution.py:25
  25.0 5.6 %copy-start = (f32[4096]{0:T(1024)S(1)}, f32[4096]{0:T(1024)}, u32[]{:S(2)}) copy-start(f32[4096]{0:T(1024)} %param.13) | copy-start | bytes 49156
  25.0 8.4 %collective-permute-start.15 = (bf16[128,512]{1,0:T(8,128)(2,1)S(1)}, bf16[128,512]{1,0:T(8,128)(2,1)S(1)}, u32[]{:S(2)}, u32[]{:S(2)}) collective-permute-start(bf16[128,512]{1,0:T(8,128)(2,1)S(1)} %get-tuple-element.94), channel_id=1, source_target_pairs={{0,2},{1,3},{2,0},{3,1},{4,6},{5,7},{6,4},{7,5},{8,10},{9,11},{10,... | collective-permute-start | bytes 393224 | tf_op jit(solution)/shard_map/ppermute | solution.py:25
  26.5 9.6 %collective-permute-start.13 = (bf16[128,512]{1,0:T(8,128)(2,1)S(1)}, bf16[128,512]{1,0:T(8,128)(2,1)S(1)}, u32[]{:S(2)}, u32[]{:S(2)}) collective-permute-start(bf16[128,512]{1,0:T(8,128)(2,1)S(1)} %get-tuple-element.92), channel_id=1, source_target_pairs={{0,2},{1,3},{2,0},{3,1},{4,6},{5,7},{6,4},{7,5},{8,10},{9,11},{10,... | collective-permute-start | bytes 393224 | tf_op jit(solution)/shard_map/ppermute | solution.py:25
  27.7 10.4 %collective-permute-start.10 = (bf16[128,512]{1,0:T(8,128)(2,1)S(1)}, bf16[128,512]{1,0:T(8,128)(2,1)S(1)}, u32[]{:S(2)}, u32[]{:S(2)}) collective-permute-start(bf16[128,512]{1,0:T(8,128)(2,1)S(1)} %get-tuple-element.88), channel_id=1, source_target_pairs={{0,2},{1,3},{2,0},{3,1},{4,6},{5,7},{6,4},{7,5},{8,10},{9,11},{10,... | collective-permute-start | bytes 393224 | tf_op jit(solution)/shard_map/ppermute | solution.py:25
  30.6 7.7 %collective-permute-start.18 = (bf16[128,512]{1,0:T(8,128)(2,1)S(1)}, bf16[128,512]{1,0:T(8,128)(2,1)S(1)}, u32[]{:S(2)}, u32[]{:S(2)}) collective-permute-start(bf16[128,512]{1,0:T(8,128)(2,1)S(1)} %shard_map.109.refs_1_), channel_id=1, source_target_pairs={{0,1},{1,0},{2,3},{3,2},{4,5},{5,4},{6,7},{7,6},{8,9},{9,8},{10,11... | collective-permute-start | bytes 393224 | tf_op jit(solution)/shard_map/ppermute | solution.py:25
  33.4 5.7 %collective-permute-start.16 = (bf16[128,512]{1,0:T(8,128)(2,1)S(1)}, bf16[128,512]{1,0:T(8,128)(2,1)S(1)}, u32[]{:S(2)}, u32[]{:S(2)}) collective-permute-start(bf16[128,512]{1,0:T(8,128)(2,1)S(1)} %shard_map.108.refs_1_), channel_id=1, source_target_pairs={{0,1},{1,0},{2,3},{3,2},{4,5},{5,4},{6,7},{7,6},{8,9},{9,8},{10,11... | collective-permute-start | bytes 393224 | tf_op jit(solution)/shard_map/ppermute | solution.py:25
  36.2 3.8 %collective-permute-start.14 = (bf16[128,512]{1,0:T(8,128)(2,1)S(1)}, bf16[128,512]{1,0:T(8,128)(2,1)S(1)}, u32[]{:S(2)}, u32[]{:S(2)}) collective-permute-start(bf16[128,512]{1,0:T(8,128)(2,1)S(1)} %shard_map.107.refs_1_), channel_id=1, source_target_pairs={{0,1},{1,0},{2,3},{3,2},{4,5},{5,4},{6,7},{7,6},{8,9},{9,8},{10,11... | collective-permute-start | bytes 393224 | tf_op jit(solution)/shard_map/ppermute | solution.py:25
  38.2 3.1 %collective-permute-start.11 = (bf16[128,512]{1,0:T(8,128)(2,1)S(1)}, bf16[128,512]{1,0:T(8,128)(2,1)S(1)}, u32[]{:S(2)}, u32[]{:S(2)}) collective-permute-start(bf16[128,512]{1,0:T(8,128)(2,1)S(1)} %shard_map.105.refs_1_), channel_id=1, source_target_pairs={{0,1},{1,0},{2,3},{3,2},{4,5},{5,4},{6,7},{7,6},{8,9},{9,8},{10,11... | collective-permute-start | bytes 393224 | tf_op jit(solution)/shard_map/ppermute | solution.py:25
  40.8 15.1 %copy-start.1 = (f32[1,128]{1,0:T(1,128)S(1)}, f32[1,128]{1,0:T(1,128)}, u32[]{:S(2)}) copy-start(f32[1,128]{1,0:T(1,128)} %refs_4_.3) | copy-start | bytes 1540
  41.8 6.4 %collective-permute-start.21 = (f32[128,256]{1,0:T(8,128)S(1)}, f32[128,256]{1,0:T(8,128)S(1)}, u32[]{:S(2)}, u32[]{:S(2)}) collective-permute-start(f32[128,256]{1,0:T(8,128)S(1)} %get-tuple-element.102), channel_id=1, source_target_pairs={{0,4},{4,0},{8,12},{12,8},{16,20},{20,16},{24,28},{28,24},{1,5},{5... | collective-permute-start | bytes 393224 | tf_op jit(solution)/shard_map/ppermute | solution.py:25
  42.8 7.8 %collective-permute-start.19 = (f32[128,256]{1,0:T(8,128)S(1)}, f32[128,256]{1,0:T(8,128)S(1)}, u32[]{:S(2)}, u32[]{:S(2)}) collective-permute-start(f32[128,256]{1,0:T(8,128)S(1)} %get-tuple-element.98), channel_id=1, source_target_pairs={{0,4},{4,0},{8,12},{12,8},{16,20},{20,16},{24,28},{28,24},{1,5},{5... | collective-permute-start | bytes 393224 | tf_op jit(solution)/shard_map/ppermute | solution.py:25
  48.3 6.0 %collective-permute-start.22 = (f32[128,128]{1,0:T(8,128)S(1)}, f32[128,128]{1,0:T(8,128)S(1)}, u32[]{:S(2)}, u32[]{:S(2)}) collective-permute-start(f32[128,128]{1,0:T(8,128)S(1)} %get-tuple-element.106), channel_id=1, source_target_pairs={{0,16},{4,20},{8,24},{12,28},{16,0},{20,4},{24,8},{28,12},{1,17},{... | collective-permute-start | bytes 196616 | tf_op jit(solution)/shard_map/ppermute | solution.py:25
  48.9 6.2 %collective-permute-start.23 = (f32[128,128]{1,0:T(8,128)S(1)}, f32[128,128]{1,0:T(8,128)S(1)}, u32[]{:S(2)}, u32[]{:S(2)}) collective-permute-start(f32[128,128]{1,0:T(8,128)S(1)} %get-tuple-element.107), channel_id=1, source_target_pairs={{0,24},{4,28},{8,16},{12,20},{16,8},{20,12},{24,0},{28,4},{1,25},{... | collective-permute-start | bytes 196616 | tf_op jit(solution)/shard_map/ppermute | solution.py:25
  50.6 5.3 %collective-permute-start.20 = (f32[128,128]{1,0:T(8,128)S(1)}, f32[128,128]{1,0:T(8,128)S(1)}, u32[]{:S(2)}, u32[]{:S(2)}) collective-permute-start(f32[128,128]{1,0:T(8,128)S(1)} %get-tuple-element.101), channel_id=1, source_target_pairs={{0,8},{4,12},{8,0},{12,4},{16,24},{20,28},{24,16},{28,20},{1,9},{5... | collective-permute-start | bytes 196616 | tf_op jit(solution)/shard_map/ppermute | solution.py:25
  67.2 5.1 %collective-permute-start.25 = (bf16[128,128]{1,0:T(8,128)(2,1)S(1)}, bf16[128,128]{1,0:T(8,128)(2,1)S(1)}, u32[]{:S(2)}, u32[]{:S(2)}) collective-permute-start(bf16[128,128]{1,0:T(8,128)(2,1)S(1)} %get-tuple-element.111.refs_0_), channel_id=1, source_target_pairs={{0,8},{4,12},{8,0},{12,4},{16,24},{20,28},{24,16},{28,20},{1,9},{5... | collective-permute-start | bytes 98312 | tf_op jit(solution)/shard_map/ppermute | solution.py:25
  68.0 5.8 %collective-permute-start.27 = (bf16[128,128]{1,0:T(8,128)(2,1)S(1)}, bf16[128,128]{1,0:T(8,128)(2,1)S(1)}, u32[]{:S(2)}, u32[]{:S(2)}) collective-permute-start(bf16[128,128]{1,0:T(8,128)(2,1)S(1)} %get-tuple-element.111.refs_0_), channel_id=1, source_target_pairs={{0,16},{4,20},{8,24},{12,28},{16,0},{20,4},{24,8},{28,12},{1,17},{... | collective-permute-start | bytes 98312 | tf_op jit(solution)/shard_map/ppermute | solution.py:25
  69.2 5.7 %collective-permute-start.29 = (bf16[128,128]{1,0:T(8,128)(2,1)S(1)}, bf16[128,128]{1,0:T(8,128)(2,1)S(1)}, u32[]{:S(2)}, u32[]{:S(2)}) collective-permute-start(bf16[128,128]{1,0:T(8,128)(2,1)S(1)} %get-tuple-element.111.refs_0_), channel_id=1, source_target_pairs={{0,24},{4,28},{8,16},{12,20},{16,8},{20,12},{24,0},{28,4},{1,25},{... | collective-permute-start | bytes 98312 | tf_op jit(solution)/shard_map/ppermute | solution.py:25
  71.7 4.3 %collective-permute-start.24 = (bf16[128,128]{1,0:T(8,128)(2,1)S(1)}, bf16[128,128]{1,0:T(8,128)(2,1)S(1)}, u32[]{:S(2)}, u32[]{:S(2)}) collective-permute-start(bf16[128,128]{1,0:T(8,128)(2,1)S(1)} %get-tuple-element.111.refs_0_), channel_id=1, source_target_pairs={{0,4},{4,0},{8,12},{12,8},{16,20},{20,16},{24,28},{28,24},{1,5},{5... | collective-permute-start | bytes 98312 | tf_op jit(solution)/shard_map/ppermute | solution.py:25
  72.4 4.2 %collective-permute-start.26 = (bf16[128,128]{1,0:T(8,128)(2,1)S(1)}, bf16[128,128]{1,0:T(8,128)(2,1)S(1)}, u32[]{:S(2)}, u32[]{:S(2)}) collective-permute-start(bf16[128,128]{1,0:T(8,128)(2,1)S(1)} %collective-permute-done.25.refs_2_), channel_id=1, source_target_pairs={{0,4},{4,0},{8,12},{12,8},{16,20},{20,16},{24,28},{28,24},{1,5},{5... | collective-permute-start | bytes 98312 | tf_op jit(solution)/shard_map/ppermute | solution.py:25
  73.7 3.9 %collective-permute-start.28 = (bf16[128,128]{1,0:T(8,128)(2,1)S(1)}, bf16[128,128]{1,0:T(8,128)(2,1)S(1)}, u32[]{:S(2)}, u32[]{:S(2)}) collective-permute-start(bf16[128,128]{1,0:T(8,128)(2,1)S(1)} %collective-permute-done.27.refs_4_), channel_id=1, source_target_pairs={{0,4},{4,0},{8,12},{12,8},{16,20},{20,16},{24,28},{28,24},{1,5},{5... | collective-permute-start | bytes 98312 | tf_op jit(solution)/shard_map/ppermute | solution.py:25
  74.9 3.9 %collective-permute-start.30 = (bf16[128,128]{1,0:T(8,128)(2,1)S(1)}, bf16[128,128]{1,0:T(8,128)(2,1)S(1)}, u32[]{:S(2)}, u32[]{:S(2)}) collective-permute-start(bf16[128,128]{1,0:T(8,128)(2,1)S(1)} %collective-permute-done.29.refs_6_), channel_id=1, source_target_pairs={{0,4},{4,0},{8,12},{12,8},{16,20},{20,16},{24,28},{28,24},{1,5},{5... | collective-permute-start | bytes 98312 | tf_op jit(solution)/shard_map/ppermute | solution.py:25
  79.2 1.4 %collective-permute-start.32 = (bf16[128,512]{1,0:T(8,128)(2,1)S(1)}, bf16[128,512]{1,0:T(8,128)(2,1)S(1)}, u32[]{:S(2)}, u32[]{:S(2)}) collective-permute-start(bf16[128,512]{1,0:T(8,128)(2,1)S(1)} %shard_map.122), channel_id=1, source_target_pairs={{0,1},{1,0},{2,3},{3,2},{4,5},{5,4},{6,7},{7,6},{8,9},{9,8},{10,11... | collective-permute-start | bytes 393224 | tf_op jit(solution)/shard_map/ppermute | solution.py:25
  79.6 1.9 %collective-permute-start.31 = (bf16[128,512]{1,0:T(8,128)(2,1)S(1)}, bf16[128,512]{1,0:T(8,128)(2,1)S(1)}, u32[]{:S(2)}, u32[]{:S(2)}) collective-permute-start(bf16[128,512]{1,0:T(8,128)(2,1)S(1)} %shard_map.121), channel_id=1, source_target_pairs={{0,1},{1,0},{2,3},{3,2},{4,5},{5,4},{6,7},{7,6},{8,9},{9,8},{10,11... | collective-permute-start | bytes 393224 | tf_op jit(solution)/shard_map/ppermute | solution.py:25
  81.3 3.3 %collective-permute-start.36 = (bf16[128,512]{1,0:T(8,128)(2,1)S(1)}, bf16[128,512]{1,0:T(8,128)(2,1)S(1)}, u32[]{:S(2)}, u32[]{:S(2)}) collective-permute-start(bf16[128,512]{1,0:T(8,128)(2,1)S(1)} %shard_map.124), channel_id=1, source_target_pairs={{0,1},{1,0},{2,3},{3,2},{4,5},{5,4},{6,7},{7,6},{8,9},{9,8},{10,11... | collective-permute-start | bytes 393224 | tf_op jit(solution)/shard_map/ppermute | solution.py:25
  82.2 3.2 %collective-permute-start.33 = (bf16[128,512]{1,0:T(8,128)(2,1)S(1)}, bf16[128,512]{1,0:T(8,128)(2,1)S(1)}, u32[]{:S(2)}, u32[]{:S(2)}) collective-permute-start(bf16[128,512]{1,0:T(8,128)(2,1)S(1)} %shard_map.126), channel_id=1, source_target_pairs={{0,1},{1,0},{2,3},{3,2},{4,5},{5,4},{6,7},{7,6},{8,9},{9,8},{10,11... | collective-permute-start | bytes 393224 | tf_op jit(solution)/shard_map/ppermute | solution.py:25
  82.6 6.4 %collective-permute-start.41 = (bf16[128,512]{1,0:T(8,128)(2,1)S(1)}, bf16[128,512]{1,0:T(8,128)(2,1)S(1)}, u32[]{:S(2)}, u32[]{:S(2)}) collective-permute-start(bf16[128,512]{1,0:T(8,128)(2,1)S(1)} %get-tuple-element.128), channel_id=1, source_target_pairs={{0,2},{1,3},{2,0},{3,1},{4,6},{5,7},{6,4},{7,5},{8,10},{9,11},{10,... | collective-permute-start | bytes 393224 | tf_op jit(solution)/shard_map/ppermute | solution.py:25
  83.0 8.8 %collective-permute-start.39 = (bf16[128,512]{1,0:T(8,128)(2,1)S(1)}, bf16[128,512]{1,0:T(8,128)(2,1)S(1)}, u32[]{:S(2)}, u32[]{:S(2)}) collective-permute-start(bf16[128,512]{1,0:T(8,128)(2,1)S(1)} %get-tuple-element.126), channel_id=1, source_target_pairs={{0,2},{1,3},{2,0},{3,1},{4,6},{5,7},{6,4},{7,5},{8,10},{9,11},{10,... | collective-permute-start | bytes 393224 | tf_op jit(solution)/shard_map/ppermute | solution.py:25
  85.0 9.6 %collective-permute-start.37 = (bf16[128,512]{1,0:T(8,128)(2,1)S(1)}, bf16[128,512]{1,0:T(8,128)(2,1)S(1)}, u32[]{:S(2)}, u32[]{:S(2)}) collective-permute-start(bf16[128,512]{1,0:T(8,128)(2,1)S(1)} %get-tuple-element.124), channel_id=1, source_target_pairs={{0,2},{1,3},{2,0},{3,1},{4,6},{5,7},{6,4},{7,5},{8,10},{9,11},{10,... | collective-permute-start | bytes 393224 | tf_op jit(solution)/shard_map/ppermute | solution.py:25
  85.7 10.8 %collective-permute-start.34 = (bf16[128,512]{1,0:T(8,128)(2,1)S(1)}, bf16[128,512]{1,0:T(8,128)(2,1)S(1)}, u32[]{:S(2)}, u32[]{:S(2)}) collective-permute-start(bf16[128,512]{1,0:T(8,128)(2,1)S(1)} %get-tuple-element.120), channel_id=1, source_target_pairs={{0,2},{1,3},{2,0},{3,1},{4,6},{5,7},{6,4},{7,5},{8,10},{9,11},{10,... | collective-permute-start | bytes 393224 | tf_op jit(solution)/shard_map/ppermute | solution.py:25
  89.0 7.7 %collective-permute-start.42 = (bf16[128,512]{1,0:T(8,128)(2,1)S(1)}, bf16[128,512]{1,0:T(8,128)(2,1)S(1)}, u32[]{:S(2)}, u32[]{:S(2)}) collective-permute-start(bf16[128,512]{1,0:T(8,128)(2,1)S(1)} %shard_map.132.refs_1_), channel_id=1, source_target_pairs={{0,1},{1,0},{2,3},{3,2},{4,5},{5,4},{6,7},{7,6},{8,9},{9,8},{10,11... | collective-permute-start | bytes 393224 | tf_op jit(solution)/shard_map/ppermute | solution.py:25
  91.8 5.7 %collective-permute-start.40 = (bf16[128,512]{1,0:T(8,128)(2,1)S(1)}, bf16[128,512]{1,0:T(8,128)(2,1)S(1)}, u32[]{:S(2)}, u32[]{:S(2)}) collective-permute-start(bf16[128,512]{1,0:T(8,128)(2,1)S(1)} %shard_map.131.refs_1_), channel_id=1, source_target_pairs={{0,1},{1,0},{2,3},{3,2},{4,5},{5,4},{6,7},{7,6},{8,9},{9,8},{10,11... | collective-permute-start | bytes 393224 | tf_op jit(solution)/shard_map/ppermute | solution.py:25
  94.6 3.8 %collective-permute-start.38 = (bf16[128,512]{1,0:T(8,128)(2,1)S(1)}, bf16[128,512]{1,0:T(8,128)(2,1)S(1)}, u32[]{:S(2)}, u32[]{:S(2)}) collective-permute-start(bf16[128,512]{1,0:T(8,128)(2,1)S(1)} %shard_map.130.refs_1_), channel_id=1, source_target_pairs={{0,1},{1,0},{2,3},{3,2},{4,5},{5,4},{6,7},{7,6},{8,9},{9,8},{10,11... | collective-permute-start | bytes 393224 | tf_op jit(solution)/shard_map/ppermute | solution.py:25
  96.6 3.1 %collective-permute-start.35 = (bf16[128,512]{1,0:T(8,128)(2,1)S(1)}, bf16[128,512]{1,0:T(8,128)(2,1)S(1)}, u32[]{:S(2)}, u32[]{:S(2)}) collective-permute-start(bf16[128,512]{1,0:T(8,128)(2,1)S(1)} %shard_map.128.refs_1_), channel_id=1, source_target_pairs={{0,1},{1,0},{2,3},{3,2},{4,5},{5,4},{6,7},{7,6},{8,9},{9,8},{10,11... | collective-permute-start | bytes 393224 | tf_op jit(solution)/shard_map/ppermute | solution.py:25
  100.2 6.4 %collective-permute-start.45 = (f32[128,256]{1,0:T(8,128)S(1)}, f32[128,256]{1,0:T(8,128)S(1)}, u32[]{:S(2)}, u32[]{:S(2)}) collective-permute-start(f32[128,256]{1,0:T(8,128)S(1)} %get-tuple-element.134), channel_id=1, source_target_pairs={{0,4},{4,0},{8,12},{12,8},{16,20},{20,16},{24,28},{28,24},{1,5},{5... | collective-permute-start | bytes 393224 | tf_op jit(solution)/shard_map/ppermute | solution.py:25
  101.2 8.2 %collective-permute-start.43 = (f32[128,256]{1,0:T(8,128)S(1)}, f32[128,256]{1,0:T(8,128)S(1)}, u32[]{:S(2)}, u32[]{:S(2)}) collective-permute-start(f32[128,256]{1,0:T(8,128)S(1)} %get-tuple-element.130), channel_id=1, source_target_pairs={{0,4},{4,0},{8,12},{12,8},{16,20},{20,16},{24,28},{28,24},{1,5},{5... | collective-permute-start | bytes 393224 | tf_op jit(solution)/shard_map/ppermute | solution.py:25
  106.7 7.2 %collective-permute-start.46 = (f32[128,128]{1,0:T(8,128)S(1)}, f32[128,128]{1,0:T(8,128)S(1)}, u32[]{:S(2)}, u32[]{:S(2)}) collective-permute-start(f32[128,128]{1,0:T(8,128)S(1)} %get-tuple-element.138), channel_id=1, source_target_pairs={{0,16},{4,20},{8,24},{12,28},{16,0},{20,4},{24,8},{28,12},{1,17},{... | collective-permute-start | bytes 196616 | tf_op jit(solution)/shard_map/ppermute | solution.py:25
  106.8 7.1 %collective-permute-start.47 = (f32[128,128]{1,0:T(8,128)S(1)}, f32[128,128]{1,0:T(8,128)S(1)}, u32[]{:S(2)}, u32[]{:S(2)}) collective-permute-start(f32[128,128]{1,0:T(8,128)S(1)} %get-tuple-element.139), channel_id=1, source_target_pairs={{0,24},{4,28},{8,16},{12,20},{16,8},{20,12},{24,0},{28,4},{1,25},{... | collective-permute-start | bytes 196616 | tf_op jit(solution)/shard_map/ppermute | solution.py:25
  109.4 5.1 %collective-permute-start.44 = (f32[128,128]{1,0:T(8,128)S(1)}, f32[128,128]{1,0:T(8,128)S(1)}, u32[]{:S(2)}, u32[]{:S(2)}) collective-permute-start(f32[128,128]{1,0:T(8,128)S(1)} %get-tuple-element.133), channel_id=1, source_target_pairs={{0,8},{4,12},{8,0},{12,4},{16,24},{20,28},{24,16},{28,20},{1,9},{5... | collective-permute-start | bytes 196616 | tf_op jit(solution)/shard_map/ppermute | solution.py:25
